TPU v7x, 256 devices: a whole 4x4x8 slice. The times are simulated.
256 devices in a mesh: st: 16 (over y, x), tp: 16 (over z, core).
Axes of the slice: x: 4, y: 4, z: 8, core: 2. Of those that a mesh axis runs over, the one named last changes fastest.
Arguments:
- continuous: bfloat16 [512, 3, 1424], P(('st', 'tp')), may hold values from -48 to 48
- templates: bfloat16 [512, 12, 3, 400], P(('st', 'tp')), may hold values from -120 to 120
- station_list: int32 [512, 12], P(('st', 'tp')), may hold values from 0 to 511, as said below
- moveouts: int32 [512, 12], P(('st', 'tp')), may hold values from 0 to 256
Outputs:
- detection: float32 [512, 768], P(('st', 'tp'))
Inputs may be any that keep to these rules, and one draw needn't show every extreme that they name: `station_list`: A station's group is station // 32. The 12 stations of a template are distinct, and so are their indices within their groups (station % 32). The rows of one device (2 templates, aligned blocks in order) name at most 3 stations of any one group, and in every such block one group is named exactly 3 times; blocks b and b2 with b % 16 == b2 % 16 share that group.
All inputs are finite; a program needn't handle non-finite values.
Results may differ from a plain program's by a relative error of at most 0.0003.
Values may be sent and summed in bfloat16 or wider, within the bound.
No kernel may reach another device: no remote copies, remote signals or barrier semaphores. Data moves between devices by JAX's collectives and lax.ppermute only.
A program may use at most 64 MiB of HBM per device.

v0:
```python
import math

import jax
import jax.numpy as jnp
from jax import lax
from jax.sharding import PartitionSpec as P

WIN = 768
TLEN = 400
CH = 3
OUT = 1024


EPS = 1e-05


def frame_width():
    return 128


def toeplitz(vector, row_width, frame_size):
    leading = vector.shape[:-1]
    padded = jnp.concatenate(
        [vector, jnp.zeros(leading + (row_width + 1 - vector.shape[-1],), vector.dtype)], axis=-1
    )
    repeated = jnp.tile(padded, (1,) * len(leading) + (frame_size,))
    return repeated[..., : frame_size * row_width].reshape(leading + (frame_size, row_width))


def to_frames(series, frame_size, frame_count):
    target = frame_size * frame_count
    length_now = series.shape[-1]
    if length_now >= target:
        fitted = series[..., :target]
    else:
        fitted = jnp.concatenate(
            [series, jnp.zeros(series.shape[:-1] + (target - length_now,), series.dtype)], axis=-1
        )
    return fitted.reshape(series.shape[:-1] + (frame_count, frame_size))


def inverse_level(row_data):
    squares = jnp.square(row_data.astype(jnp.float32))
    running = jnp.cumsum(squares, axis=-1)
    running = jnp.concatenate([jnp.zeros(running.shape[:-1] + (1,), jnp.float32), running], axis=-1)
    energy = running[..., TLEN : TLEN + OUT] - running[..., :OUT]
    return lax.rsqrt(energy / TLEN + EPS)


def correlate(templates, row_data, inverse, shifts):
    frame_size = frame_width()
    blocks = OUT // frame_size
    step_count = (TLEN + 2 * frame_size - 2) // frame_size
    frames = to_frames(row_data, frame_size, blocks + step_count - 1)
    bands = toeplitz(templates, step_count * frame_size, frame_size)
    running = jnp.zeros(templates.shape[:-1] + (blocks, frame_size), jnp.float32)
    for step_index in range(step_count):
        running = running + jnp.einsum(
            "ncbp,ncip->ncbi",
            frames[:, :, step_index : step_index + blocks],
            bands[..., step_index * frame_size : (step_index + 1) * frame_size],
            preferred_element_type=jnp.float32,
        )
    raw_sums = running.reshape(templates.shape[:-1] + (OUT,))
    template_values = templates.astype(jnp.float32)
    template_inverse = lax.rsqrt(jnp.mean(template_values * template_values, axis=-1) + EPS)
    scaled = raw_sums * inverse * (template_inverse / TLEN)[..., None]
    summed = jnp.sum(scaled, axis=1)
    return jax.vmap(lambda series, start_at: lax.dynamic_slice_in_dim(series, start_at, WIN))(
        summed, shifts
    )


def in_blocks(worker, arrays, item_count):
    block_size = math.gcd(item_count, 32)
    grouped = jax.tree.map(
        lambda member: member.reshape((item_count // block_size, block_size) + member.shape[1:]),
        arrays,
    )
    result = lax.map(worker, grouped)
    return result.reshape((item_count,) + result.shape[2:])


def shards(continuous, templates, station_list, moveouts):
    group_count = lax.axis_size("st")
    template_count = templates.shape[0]
    list_size = templates.shape[1]
    group_size = continuous.shape[0] * lax.axis_size("tp")
    entries = template_count * list_size
    capacity = 2 * entries // group_count
    slots_total = group_count * capacity
    flat_list = station_list.reshape(entries)
    owners = flat_list // group_size
    within = flat_list - owners * group_size
    member = (owners[:, None] == jnp.arange(group_count, dtype=jnp.int32)[None, :]).astype(
        jnp.int32
    )
    earlier = jnp.cumsum(member, axis=0) - member
    position = jnp.sum(earlier * member, axis=1)
    slot_index = owners * capacity + position
    flat_shift = moveouts.reshape(entries)
    flat_templates = templates.reshape(entries, CH, TLEN)
    group_rows = lax.all_gather(continuous, "tp", axis=0, tiled=True)
    local_scale = inverse_level(continuous)
    group_scale = lax.all_gather(local_scale, "tp", axis=0, tiled=True)
    slot_templates = (
        jnp.zeros((slots_total, CH, TLEN), jnp.bfloat16)
        .at[slot_index]
        .set(flat_templates)
        .reshape(group_count, capacity, CH, TLEN)
    )
    slot_station = (
        jnp.zeros((slots_total,), jnp.int32)
        .at[slot_index]
        .set(within)
        .reshape(group_count, capacity)
    )
    slot_shift = (
        jnp.zeros((slots_total,), jnp.int32)
        .at[slot_index]
        .set(flat_shift)
        .reshape(group_count, capacity)
    )
    template_rows = jnp.arange(entries, dtype=jnp.int32) // list_size
    slot_row = (
        jnp.full((slots_total,), -1, jnp.int32)
        .at[slot_index]
        .set(template_rows)
        .reshape(group_count, capacity)
    )
    pieces = (
        lax.all_to_all(slot_templates, "st", split_axis=0, concat_axis=0, tiled=True),
        lax.all_to_all(slot_station, "st", split_axis=0, concat_axis=0, tiled=True),
        lax.all_to_all(slot_shift, "st", split_axis=0, concat_axis=0, tiled=True),
        lax.all_to_all(slot_row, "st", split_axis=0, concat_axis=0, tiled=True),
    )
    given_items = pieces[1].shape[1]
    item_total = group_count * given_items
    stations = pieces[1].reshape(item_total)

    def block_work(block_parts):
        picked = group_rows[block_parts[1]]
        scales = group_scale[block_parts[1]]
        return correlate(block_parts[0], picked, scales, block_parts[2])

    aligned = in_blocks(
        block_work,
        (pieces[0].reshape(item_total, CH, TLEN), stations, pieces[2].reshape(item_total)),
        item_total,
    )
    aligned = aligned.reshape(group_count, given_items, WIN)
    outcome = lax.all_to_all(aligned, "st", split_axis=0, concat_axis=0, tiled=True)
    returned = outcome.reshape(slots_total, WIN)
    detection = jnp.sum(returned[slot_index].reshape(template_count, list_size, WIN), axis=1)
    return detection


def solution(mesh):
    placed = (
        P(("st", "tp"), None, None),
        P(("st", "tp"), None, None, None),
        P(("st", "tp"), None),
        P(("st", "tp"), None),
    )
    return jax.shard_map(
        shards, mesh=mesh, in_specs=placed, out_specs=P(("st", "tp"), None), check_vma=False
    )
```

profile of v0, /device:TPU:1, one launch (start us, length us, event | category | flops | bytes accessed | tf_op | source)
XLA Modules:
  0.0 315.8 jit_solution(9241197503857095357)
XLA Ops:
  3.2 7.6 %all-to-all-start = ((s32[16,1,3]{2,1,0:T(1,128)}), s32[16,1,3]{2,1,0:T(1,128)S(1)}, u32[]{:S(2)}, u32[]{:S(2)}) async-start(s32[16,1,3]{2,1,0:T(1,128)} %bitcast.7), calls=%async_computation | async-start | bytes 16384 | tf_op jit(solution)/shard_map/all_to_all | solution.py:133
  13.8 1.7 reduce-window.6
  16.6 22.2 %all_gather.7 = f32[32,3,1024]{2,1,0:T(4,128)S(1)} all-gather(f32[2,3,1024]{2,1,0:T(4,128)S(1)} %copy.76), channel_id=1, replica_groups=mesh['st'=16,'tp'=16] {'tp'}, dimensions={0}, use_global_device_ids=true | all-gather | bytes 417792 | tf_op jit(solution)/shard_map/all_gather | solution.py:105
  39.6 6.9 %all-to-all-start.2 = ((s32[16,1,3]{2,1,0:T(1,128)}), s32[16,1,3]{2,1,0:T(1,128)S(1)}, u32[]{:S(2)}, u32[]{:S(2)}) async-start(s32[16,1,3]{2,1,0:T(1,128)} %bitcast.11), calls=%async_computation.2 | async-start | bytes 16384 | tf_op jit(solution)/shard_map/all_to_all | solution.py:134
  46.6 1.5 scatter_fusion
  48.9 3.9 %all-to-all-done.2 = s32[16,1,3]{2,1,0:T(1,128)S(1)} async-done(((s32[16,1,3]{2,1,0:T(1,128)}), s32[16,1,3]{2,1,0:T(1,128)S(1)}, u32[]{:S(2)}, u32[]{:S(2)}) %all-to-all-start.2) | async-done | bytes 224 | tf_op jit(solution)/shard_map/all_to_all | solution.py:134
  52.8 3.5 %all-to-all-start.1 = ((bf16[16,3,3,400]{3,1,2,0:T(4,128)(2,1)}), bf16[16,3,3,400]{3,1,2,0:T(4,128)(2,1)S(1)}, u32[]{:S(2)}, u32[]{:S(2)}) async-start(bf16[16,3,3,400]{3,1,2,0:T(4,128)(2,1)} %copy.70), calls=%async_computation.1 | async-start | bytes 393216 | tf_op jit(solution)/shard_map/all_to_all | solution.py:132
  56.3 16.9 %all_gather.6 = bf16[32,3,1424]{2,1,0:T(4,128)(2,1)S(1)} all-gather(bf16[2,3,1424]{2,1,0:T(4,128)(2,1)S(1)} %copy.67), channel_id=1, replica_groups=mesh['st'=16,'tp'=16] {'tp'}, dimensions={0}, use_global_device_ids=true | all-gather | bytes 290496 | tf_op jit(solution)/shard_map/all_gather | solution.py:103
  75.9 222.4 %while.13 = (s32[]{:T(128)}, f32[3,16,768]{2,1,0:T(8,128)}, s32[3,16]{1,0:T(4,128)S(1)}, bf16[32,3,1424]{2,1,0:T(4,128)(2,1)S(1)}, bf16[3,16,3,400]{3,1,0,2:T(8,...) while((s32[]{:T(128)}, f32[3,16,768]{2,1,0:T(8,128)}, ...), condition=%wide.region_10.11_spmd, body=%wide.region_7.10_spmd.sunk | while | flops 63301088 | bytes 91004616 | solution.py:80
  77.8 4.3 %tile.11 = bf16[16,3,128,641]{3,2,0,1:T(8,128)(2,1)} broadcast(bf16[16,3,641]{2,0,1:T(8,128)(2,1)S(1)} %concatenate.21), dimensions={0,1,3} | broadcast | bytes 7938144 | tf_op jit(solution)/shard_map/while/body/eval_jaxpr/tile | solution.py:26
  82.1 14.9 %tile.12 = bf16[16,3,82048]{2,0,1:T(8,128)(2,1)} reshape(bf16[16,3,128,641]{3,2,0,1:T(8,128)(2,1)} %tile.11) | data formatting | bytes 15753216 | tf_op jit(solution)/shard_map/while/body/eval_jaxpr/tile | solution.py:26
  97.0 3.2 %slice-done = bf16[16,3,81920]{2,0,1:T(8,128)(2,1)S(1)} async-done(((bf16[16,3,82048]{2,0,1:T(8,128)(2,1)}), bf16[16,3,81920]{2,0,1:T(8,128)(2,1)S(1)}, s32[]{:S(2)}) %slice-start) | async-done | bytes 7864344 | tf_op jit(solution)/shard_map/while/body/eval_jaxpr/slice | solution.py:27
  100.2 4.6 %copy.136 = bf16[6,8,128,640]{3,2,1,0:T(8,128)(2,1)} copy(bf16[6,8,128,640]{3,1,2,0:T(8,128)(2,1)S(1)} %bitcast.72) | data formatting | bytes 15728640 | tf_op jit(solution)/shard_map/while
  104.8 3.7 %fusion.78 = (bf16[16,3,128,128]{3,2,0,1:T(8,128)(2,1)S(1)}, bf16[16,3,128,128]{3,2,0,1:T(8,128)(2,1)S(1)}, bf16[16,3,128,128]{3,2,0,1:T(8,128)(2,1)S(1)}, bf16[...) fusion(bf16[16,3,128,640]{3,2,0,1:T(8,128)(2,1)} %bitcast.73), kind=kLoop, calls=%fused_computation.70.clone.1 | loop fusion | bytes 15728640 | tf_op jit(solution)/shard_map/while/body/eval_jaxpr/slice | solution.py:61
  114.1 35.3 %while.14 = (s32[]{:T(128)}, f32[16,1024]{1,0:T(8,128)S(1)}, s32[16,2]{0,1:T(2,128)S(1)}, f32[16,768]{1,0:T(8,128)S(1)}, s32[]{:T(128)}, /*index=5*/s32[]{:T(128)}) while((s32[]{:T(128)}, f32[16,1024]{1,0:T(8,128)S(1)}, s32[16,2]{0,1:T(2,128)S(1)}, f32[16,768]{1,0:T(8,128)S(1)}, s32[]{:T(128)}, /*index=5*/s32[]{:T(128)}) %tuple.55), condition=%wide.while_cond, body=%wide.while_body.sunk | while | flops 2 | bytes 12401 | solution.py:69
  114.8 1.5 dynamic-slice.7
  117.0 1.5 dynamic-slice.7
  119.2 1.5 dynamic-slice.7
  121.4 1.5 dynamic-slice.7
  123.6 1.5 dynamic-slice.7
  125.9 1.5 dynamic-slice.7
  128.1 1.5 dynamic-slice.7
  130.3 1.5 dynamic-slice.7
  132.5 1.5 dynamic-slice.7
  134.7 1.5 dynamic-slice.7
  136.9 1.5 dynamic-slice.7
  139.1 1.5 dynamic-slice.7
  141.3 1.5 dynamic-slice.7
  143.5 1.5 dynamic-slice.7
  145.7 1.5 dynamic-slice.7
  147.9 1.5 dynamic-slice.7
  152.0 4.3 %tile.11 = bf16[16,3,128,641]{3,2,0,1:T(8,128)(2,1)} broadcast(bf16[16,3,641]{2,0,1:T(8,128)(2,1)S(1)} %concatenate.21), dimensions={0,1,3} | broadcast | bytes 7938144 | tf_op jit(solution)/shard_map/while/body/eval_jaxpr/tile | solution.py:26
  156.2 14.9 %tile.12 = bf16[16,3,82048]{2,0,1:T(8,128)(2,1)} reshape(bf16[16,3,128,641]{3,2,0,1:T(8,128)(2,1)} %tile.11) | data formatting | bytes 15753216 | tf_op jit(solution)/shard_map/while/body/eval_jaxpr/tile | solution.py:26
  171.1 3.2 %slice-done = bf16[16,3,81920]{2,0,1:T(8,128)(2,1)S(1)} async-done(((bf16[16,3,82048]{2,0,1:T(8,128)(2,1)}), bf16[16,3,81920]{2,0,1:T(8,128)(2,1)S(1)}, s32[]{:S(2)}) %slice-start) | async-done | bytes 7864344 | tf_op jit(solution)/shard_map/while/body/eval_jaxpr/slice | solution.py:27
  174.4 4.6 %copy.136 = bf16[6,8,128,640]{3,2,1,0:T(8,128)(2,1)} copy(bf16[6,8,128,640]{3,1,2,0:T(8,128)(2,1)S(1)} %bitcast.72) | data formatting | bytes 15728640 | tf_op jit(solution)/shard_map/while
  178.9 3.7 %fusion.78 = (bf16[16,3,128,128]{3,2,0,1:T(8,128)(2,1)S(1)}, bf16[16,3,128,128]{3,2,0,1:T(8,128)(2,1)S(1)}, bf16[16,3,128,128]{3,2,0,1:T(8,128)(2,1)S(1)}, bf16[...) fusion(bf16[16,3,128,640]{3,2,0,1:T(8,128)(2,1)} %bitcast.73), kind=kLoop, calls=%fused_computation.70.clone.1 | loop fusion | bytes 15728640 | tf_op jit(solution)/shard_map/while/body/eval_jaxpr/slice | solution.py:61
  188.3 35.3 %while.14 = (s32[]{:T(128)}, f32[16,1024]{1,0:T(8,128)S(1)}, s32[16,2]{0,1:T(2,128)S(1)}, f32[16,768]{1,0:T(8,128)S(1)}, s32[]{:T(128)}, /*index=5*/s32[]{:T(128)}) while((s32[]{:T(128)}, f32[16,1024]{1,0:T(8,128)S(1)}, s32[16,2]{0,1:T(2,128)S(1)}, f32[16,768]{1,0:T(8,128)S(1)}, s32[]{:T(128)}, /*index=5*/s32[]{:T(128)}) %tuple.55), condition=%wide.while_cond, body=%wide.while_body.sunk | while | flops 2 | bytes 12401 | solution.py:69
  189.0 1.5 dynamic-slice.7
  191.2 1.5 dynamic-slice.7
  193.4 1.5 dynamic-slice.7
  195.6 1.5 dynamic-slice.7
  197.8 1.5 dynamic-slice.7
  200.0 1.5 dynamic-slice.7
  202.2 1.5 dynamic-slice.7
  204.4 1.5 dynamic-slice.7
  206.6 1.5 dynamic-slice.7
  208.8 1.5 dynamic-slice.7
  211.0 1.5 dynamic-slice.7
  213.2 1.5 dynamic-slice.7
  215.4 1.5 dynamic-slice.7
  217.7 1.5 dynamic-slice.7
  219.9 1.5 dynamic-slice.7
  226.1 4.3 %tile.11 = bf16[16,3,128,641]{3,2,0,1:T(8,128)(2,1)} broadcast(bf16[16,3,641]{2,0,1:T(8,128)(2,1)S(1)} %concatenate.21), dimensions={0,1,3} | broadcast | bytes 7938144 | tf_op jit(solution)/shard_map/while/body/eval_jaxpr/tile | solution.py:26
  230.4 14.9 %tile.12 = bf16[16,3,82048]{2,0,1:T(8,128)(2,1)} reshape(bf16[16,3,128,641]{3,2,0,1:T(8,128)(2,1)} %tile.11) | data formatting | bytes 15753216 | tf_op jit(solution)/shard_map/while/body/eval_jaxpr/tile | solution.py:26
  245.3 3.2 %slice-done = bf16[16,3,81920]{2,0,1:T(8,128)(2,1)S(1)} async-done(((bf16[16,3,82048]{2,0,1:T(8,128)(2,1)}), bf16[16,3,81920]{2,0,1:T(8,128)(2,1)S(1)}, s32[]{:S(2)}) %slice-start) | async-done | bytes 7864344 | tf_op jit(solution)/shard_map/while/body/eval_jaxpr/slice | solution.py:27
  248.5 4.6 %copy.136 = bf16[6,8,128,640]{3,2,1,0:T(8,128)(2,1)} copy(bf16[6,8,128,640]{3,1,2,0:T(8,128)(2,1)S(1)} %bitcast.72) | data formatting | bytes 15728640 | tf_op jit(solution)/shard_map/while
  253.1 3.7 %fusion.78 = (bf16[16,3,128,128]{3,2,0,1:T(8,128)(2,1)S(1)}, bf16[16,3,128,128]{3,2,0,1:T(8,128)(2,1)S(1)}, bf16[16,3,128,128]{3,2,0,1:T(8,128)(2,1)S(1)}, bf16[...) fusion(bf16[16,3,128,640]{3,2,0,1:T(8,128)(2,1)} %bitcast.73), kind=kLoop, calls=%fused_computation.70.clone.1 | loop fusion | bytes 15728640 | tf_op jit(solution)/shard_map/while/body/eval_jaxpr/slice | solution.py:61
  262.4 35.3 %while.14 = (s32[]{:T(128)}, f32[16,1024]{1,0:T(8,128)S(1)}, s32[16,2]{0,1:T(2,128)S(1)}, f32[16,768]{1,0:T(8,128)S(1)}, s32[]{:T(128)}, /*index=5*/s32[]{:T(128)}) while((s32[]{:T(128)}, f32[16,1024]{1,0:T(8,128)S(1)}, s32[16,2]{0,1:T(2,128)S(1)}, f32[16,768]{1,0:T(8,128)S(1)}, s32[]{:T(128)}, /*index=5*/s32[]{:T(128)}) %tuple.55), condition=%wide.while_cond, body=%wide.while_body.sunk | while | flops 2 | bytes 12401 | solution.py:69
  271.9 1.5 dynamic-slice.7
  283.0 1.5 dynamic-slice.7
  294.0 1.5 dynamic-slice.7
  298.4 1.6 reshape_reshape.15
  300.0 6.9 %all-to-all-start.3 = ((f32[16,3,768]{2,1,0:T(4,128)}), f32[16,3,768]{2,1,0:T(4,128)S(1)}, u32[]{:S(2)}, u32[]{:S(2)}) async-start(f32[16,3,768]{2,1,0:T(4,128)} %reshape_reshape.15), calls=%async_computation.3 | async-start | bytes 393216 | tf_op jit(solution)/shard_map/all_to_all | solution.py:152
  306.9 7.6 %all-to-all-done.3 = f32[16,3,768]{2,1,0:T(4,128)S(1)} async-done(((f32[16,3,768]{2,1,0:T(4,128)}), f32[16,3,768]{2,1,0:T(4,128)S(1)}, u32[]{:S(2)}, u32[]{:S(2)}) %all-to-all-start.3) | async-done | bytes 147488 | tf_op jit(solution)/shard_map/all_to_all | solution.py:152
  (274 shorter events, 92.3 us)
Async XLA Ops:
  0.0 39.5 %copy-start = (bf16[2,12,3,400]{3,0,2,1:T(2,128)(2,1)S(1)}, bf16[2,12,3,400]{3,0,2,1:T(2,128)(2,1)}, u32[]{:S(2)}) copy-start(bf16[2,12,3,400]{3,0,2,1:T(2,128)(2,1)} %param.7) | copy-start | bytes 172804
  3.2 36.3 %all-to-all-start = ((s32[16,1,3]{2,1,0:T(1,128)}), s32[16,1,3]{2,1,0:T(1,128)S(1)}, u32[]{:S(2)}, u32[]{:S(2)}) async-start(s32[16,1,3]{2,1,0:T(1,128)} %bitcast.7), calls=%async_computation | async-start | bytes 16384 | tf_op jit(solution)/shard_map/all_to_all | solution.py:133
  39.6 13.2 %all-to-all-start.2 = ((s32[16,1,3]{2,1,0:T(1,128)}), s32[16,1,3]{2,1,0:T(1,128)S(1)}, u32[]{:S(2)}, u32[]{:S(2)}) async-start(s32[16,1,3]{2,1,0:T(1,128)} %bitcast.11), calls=%async_computation.2 | async-start | bytes 16384 | tf_op jit(solution)/shard_map/all_to_all | solution.py:134
  52.8 22.3 %all-to-all-start.1 = ((bf16[16,3,3,400]{3,1,2,0:T(4,128)(2,1)}), bf16[16,3,3,400]{3,1,2,0:T(4,128)(2,1)S(1)}, u32[]{:S(2)}, u32[]{:S(2)}) async-start(bf16[16,3,3,400]{3,1,2,0:T(4,128)(2,1)} %copy.70), calls=%async_computation.1 | async-start | bytes 393216 | tf_op jit(solution)/shard_map/all_to_all | solution.py:132
  97.0 3.2 %slice-start = ((bf16[16,3,82048]{2,0,1:T(8,128)(2,1)}), bf16[16,3,81920]{2,0,1:T(8,128)(2,1)S(1)}, s32[]{:S(2)}) async-start(bf16[16,3,82048]{2,0,1:T(8,128)(2,1)} %tile.12), calls=%async_computation.4 | async-start | bytes 15728640 | tf_op jit(solution)/shard_map/while/body/eval_jaxpr/slice | solution.py:27
  171.1 3.2 %slice-start = ((bf16[16,3,82048]{2,0,1:T(8,128)(2,1)}), bf16[16,3,81920]{2,0,1:T(8,128)(2,1)S(1)}, s32[]{:S(2)}) async-start(bf16[16,3,82048]{2,0,1:T(8,128)(2,1)} %tile.12), calls=%async_computation.4 | async-start | bytes 15728640 | tf_op jit(solution)/shard_map/while/body/eval_jaxpr/slice | solution.py:27
  245.3 3.2 %slice-start = ((bf16[16,3,82048]{2,0,1:T(8,128)(2,1)}), bf16[16,3,81920]{2,0,1:T(8,128)(2,1)S(1)}, s32[]{:S(2)}) async-start(bf16[16,3,82048]{2,0,1:T(8,128)(2,1)} %tile.12), calls=%async_computation.4 | async-start | bytes 15728640 | tf_op jit(solution)/shard_map/while/body/eval_jaxpr/slice | solution.py:27
  300.0 14.5 %all-to-all-start.3 = ((f32[16,3,768]{2,1,0:T(4,128)}), f32[16,3,768]{2,1,0:T(4,128)S(1)}, u32[]{:S(2)}, u32[]{:S(2)}) async-start(f32[16,3,768]{2,1,0:T(4,128)} %reshape_reshape.15), calls=%async_computation.3 | async-start | bytes 393216 | tf_op jit(solution)/shard_map/all_to_all | solution.py:152
where the time goes:
time: 318 us; the launch traced here: 316 us
  local copies, waits for them, and re-layouts  217 us (68%)
  blocking collectives  39.1 us (12%)
  starting transfers between devices  24.9 us (8%)
  matrix products  13.8 us (4%)
  waiting for transfers between devices  11.5 us (4%)
  other arithmetic  8.16 us (3%)
    gather x192, local copies, waits for them, and re-layouts  105 us
    another operation x6, local copies, waits for them, and re-layouts, toeplitz(): repeated = jnp.tile(padded, (1,) * len(leading) + (frame_size,))  57.4 us
    all_gather x1, blocking collectives, shards(): group_scale = lax.all_gather(local_scale, 'tp', axis=0, tiled=True)  22.2 us
    all_gather x1, blocking collectives, shards(): group_rows = lax.all_gather(continuous, 'tp', axis=0, tiled=True)  16.9 us
    dot_general x15, matrix products, correlate(): jnp.einsum('ncbp,ncip->ncbi', frames[:, :, step_index:step_index + blocks...  13.8 us
    while x9, local copies, waits for them, and re-layouts  13.8 us
    slice x3, local copies, waits for them, and re-layouts, correlate(): bands[..., step_index * frame_size:(step_index + 1) * frame_size]  11.2 us
    slice x6, local copies, waits for them, and re-layouts, toeplitz(): repeated[..., :frame_size * row_width]  9.7 us
  transfers between devices with their start and end apart: 4, of which 2 were waited for; matrix products, arithmetic and copies ran while one was open for 3% of the time, Pallas kernels for 0%

commit v1 on v0

v1 whole, which is shorter than its diff:
```python
import jax
import jax.numpy as jnp
from jax import lax
from jax.experimental import pallas as pl
from jax.experimental.pallas import tpu as pltpu
from jax.sharding import PartitionSpec as P

WIN = 768
TLEN = 400
CH = 3
DLEN = 1424
EPS = 1e-05
LANES = 128
TILES = 12
ROWS = 40
CAP = 3
HALF = 64
DEPTH = 512
BLOCKS = WIN // LANES


def prepare(groups, entries, station_ref, data_ref, out_ref, ask_ref, slot_ref, scratch, count):
    list_size = station_ref.shape[1]
    scratch[...] = jnp.zeros_like(scratch)
    for k in range(data_ref.shape[0]):
        x = data_ref[k].astype(jnp.float32)
        for q in range(TILES):
            width = min(LANES, DLEN - q * LANES)
            scratch[pl.ds(k * ROWS + q, CH, stride=TILES), 0:width] = x[
                :, q * LANES : q * LANES + width
            ]
    packed = scratch[...].astype(jnp.bfloat16)
    for d in range(out_ref.shape[0]):
        out_ref[d] = packed
    for g in range(groups):
        count[g] = 0
        for s in range(CAP):
            ask_ref[g, 0, s] = 0
    for e in range(entries):
        station = station_ref[e // list_size, e % list_size]
        g = station // 32
        position = jnp.minimum(count[g], CAP - 1)
        count[g] = position + 1
        ask_ref[g, 0, position] = station - g * 32
        slot_ref[0, e] = g * CAP + position


def build_bands(entries, templates_ref, band_ref, scale_ref, ones_ref, scratch):
    scratch[...] = jnp.zeros_like(scratch)

    def step(e, carry):
        x = templates_ref[e].astype(jnp.float32)
        scratch[0:CH, 0:TLEN] = x
        energy = jnp.sum(x * x, axis=1, keepdims=True)
        scale = lax.rsqrt(energy / TLEN + EPS) / TLEN
        scale_ref[e] = jnp.broadcast_to(scale, (CH, LANES))
        for c in range(CH):
            rows = jnp.broadcast_to(scratch[c : c + 1, :], (HALF, DEPTH))
            band = pltpu.roll(rows, 0, 1, stride=1, stride_axis=0)
            band_ref[c, pl.ds(pl.multiple_of(e * HALF, HALF), HALF), :] = band.astype(jnp.bfloat16)
        return carry

    lax.fori_loop(0, entries, step, 0)
    r = lax.broadcasted_iota(jnp.int32, (LANES, LANES), 0)
    i = lax.broadcasted_iota(jnp.int32, (LANES, LANES), 1)
    kinds = (r >= i, r >= 0, r - i < TLEN - 384, r - i < TLEN - 512)
    for n, kind in enumerate(kinds):
        block = jnp.where(kind, 1.0, 0.0).astype(jnp.bfloat16)
        ones_ref[0:LANES, n * LANES : (n + 1) * LANES] = block
        ones_ref[LANES : 2 * LANES, n * LANES : (n + 1) * LANES] = block


def pick(groups, ask_ref, data_ref, out_ref, sem):
    for i in range(groups):
        for s in range(CAP):
            station = ask_ref[i, 0, s]
            t = station // 2
            k = station - t * 2
            pltpu.make_async_copy(
                data_ref.at[t, pl.ds(pl.multiple_of(k * ROWS, 8), ROWS)],
                out_ref.at[i, pl.ds(s * ROWS, ROWS)],
                sem,
            ).start()
    pltpu.make_async_copy(out_ref, out_ref, sem).wait()


def correlate(
    entries, slot_ref, shift_ref, data_ref, band_ref, scale_ref, ones_ref, out_ref,
    wide, shifted, squares, sums,
):
    groups, rows, _ = data_ref.shape
    list_size = entries // out_ref.shape[0]
    for g in range(groups):
        wide[g * rows : (g + 1) * rows, :] = data_ref[g].astype(jnp.float32)
    wide[groups * rows :, :] = jnp.zeros((wide.shape[0] - groups * rows, LANES), jnp.float32)
    lane = lax.broadcasted_iota(jnp.int32, (ROWS, LANES), 1)
    lane8 = lax.broadcasted_iota(jnp.int32, (8, LANES), 1)
    for e in range(entries):
        shift = shift_ref[e // list_size, e % list_size]
        base = slot_ref[0, e] * ROWS
        for h in range(2):
            moved = shift + h * HALF
            whole = moved // LANES
            part = moved - whole * LANES
            back = jnp.where(part == 0, 0, LANES - part)
            first = pltpu.roll(wide[pl.ds(base + whole, ROWS), :], back, 1)
            second = pltpu.roll(wide[pl.ds(base + whole + 1, ROWS), :], back, 1)
            y = jnp.where(lane < LANES - part, first, second)
            shifted[h, e * ROWS : (e + 1) * ROWS, :] = y
            if h == 0:
                sq = y * y
                high = sq.astype(jnp.bfloat16)
                squares[e * ROWS : (e + 1) * ROWS, 0:LANES] = high
                squares[e * ROWS : (e + 1) * ROWS, LANES:] = (
                    sq - high.astype(jnp.float32)
                ).astype(jnp.bfloat16)
    sums[...] = jnp.dot(squares[...], ones_ref[...], preferred_element_type=jnp.float32)
    totals = [jnp.zeros((8, LANES), jnp.float32) for _ in range(out_ref.shape[0])]
    for quad in range(entries // 4):
        for c in range(CH):
            frames = []
            for n in range(4):
                start = (quad * 4 + n) * ROWS + c * TILES
                for h in range(2):
                    frames.append(
                        jnp.concatenate(
                            [
                                shifted[h, start + q : start + q + 8, :]
                                for q in range(DEPTH // LANES)
                            ],
                            axis=1,
                        )
                    )
            left = jnp.concatenate(frames, axis=0).astype(jnp.bfloat16)
            product = lax.dot_general(
                left,
                band_ref[c, quad * 4 * HALF : (quad + 1) * 4 * HALF, :],
                (((1,), (1,)), ((), ())),
                preferred_element_type=jnp.float32,
            )
            for n in range(4):
                e = quad * 4 + n
                column = (n // 2) * LANES
                low = product[n * 16 : n * 16 + 8, column : column + LANES]
                high = product[n * 16 + 8 : n * 16 + 16, column : column + LANES]
                if n % 2 == 0:
                    high = pltpu.roll(high, HALF, 1)
                else:
                    low = pltpu.roll(low, HALF, 1)
                raw = jnp.where(lane8 < HALF, low, high)
                start = e * ROWS + c * TILES
                energy = (
                    sums[start : start + 8, 0:LANES]
                    + sums[start + 1 : start + 9, LANES : 2 * LANES]
                    + sums[start + 2 : start + 10, LANES : 2 * LANES]
                    + sums[start + 3 : start + 11, 2 * LANES : 3 * LANES]
                    + sums[start + 4 : start + 12, 3 * LANES :]
                )
                level = lax.rsqrt(energy / TLEN + EPS)
                totals[e // list_size] = totals[e // list_size] + raw * level * scale_ref[e][
                    c : c + 1, :
                ]
    for t, total in enumerate(totals):
        for b in range(BLOCKS):
            out_ref[t : t + 1, b * LANES : (b + 1) * LANES] = total[b : b + 1, :]


def shards(continuous, templates, station_list, moveouts):
    groups = lax.axis_size("st")
    peers = lax.axis_size("tp")
    owned = continuous.shape[0]
    template_count, list_size = station_list.shape
    entries = template_count * list_size
    smem = pl.BlockSpec(memory_space=pltpu.SMEM)
    vmem = pl.BlockSpec(memory_space=pltpu.VMEM)
    anywhere = pl.BlockSpec(memory_space=pl.ANY)

    def params():
        return pltpu.CompilerParams(vmem_limit_bytes=48 * 2**20)

    spread, asked, slots = pl.pallas_call(
        lambda *refs: prepare(groups, entries, *refs),
        out_shape=(
            jax.ShapeDtypeStruct((peers, owned * ROWS, LANES), jnp.bfloat16),
            jax.ShapeDtypeStruct((groups, 1, LANES), jnp.int32),
            jax.ShapeDtypeStruct((1, LANES), jnp.int32),
        ),
        in_specs=[smem, vmem],
        out_specs=(vmem, smem, smem),
        scratch_shapes=[
            pltpu.VMEM((owned * ROWS, LANES), jnp.float32),
            pltpu.SMEM((groups,), jnp.int32),
        ],
        compiler_params=params(),
        name="prepare",
    )(station_list, continuous)
    asks = lax.all_to_all(asked, "st", split_axis=0, concat_axis=0, tiled=True)
    group_rows = lax.all_to_all(spread, "tp", split_axis=0, concat_axis=0, tiled=True)
    bands, scales, ones = pl.pallas_call(
        lambda *refs: build_bands(entries, *refs),
        out_shape=(
            jax.ShapeDtypeStruct((CH, entries * HALF, DEPTH), jnp.bfloat16),
            jax.ShapeDtypeStruct((entries, CH, LANES), jnp.float32),
            jax.ShapeDtypeStruct((2 * LANES, 4 * LANES), jnp.bfloat16),
        ),
        in_specs=[vmem],
        out_specs=(vmem, vmem, vmem),
        scratch_shapes=[pltpu.VMEM((8, DEPTH), jnp.float32)],
        compiler_params=params(),
        name="bands",
    )(templates.reshape(entries, CH, TLEN))
    picked = pl.pallas_call(
        lambda *refs: pick(groups, *refs),
        out_shape=jax.ShapeDtypeStruct((groups, CAP * ROWS, LANES), jnp.bfloat16),
        in_specs=[smem, anywhere],
        out_specs=anywhere,
        scratch_shapes=[pltpu.SemaphoreType.DMA],
        compiler_params=params(),
        name="pick",
    )(asks, group_rows)
    records = lax.all_to_all(picked, "st", split_axis=0, concat_axis=0, tiled=True)
    return pl.pallas_call(
        lambda *refs: correlate(entries, *refs),
        out_shape=jax.ShapeDtypeStruct((template_count, WIN), jnp.float32),
        in_specs=[smem, smem, vmem, vmem, vmem, vmem],
        out_specs=vmem,
        scratch_shapes=[
            pltpu.VMEM((groups * CAP * ROWS + 8, LANES), jnp.float32),
            pltpu.VMEM((2, entries * ROWS, LANES), jnp.float32),
            pltpu.VMEM((entries * ROWS, 2 * LANES), jnp.bfloat16),
            pltpu.VMEM((entries * ROWS, 4 * LANES), jnp.float32),
        ],
        compiler_params=params(),
        name="correlate",
    )(slots, moveouts, records, bands, scales, ones)


def solution(mesh):
    placed = (
        P(("st", "tp"), None, None),
        P(("st", "tp"), None, None, None),
        P(("st", "tp"), None),
        P(("st", "tp"), None),
    )
    return jax.shard_map(
        shards, mesh=mesh, in_specs=placed, out_specs=P(("st", "tp"), None), check_vma=False
    )
```

time: 318 us -> 63.8 us (0.20)
  local copies, waits for them, and re-layouts: 217 us -> 7.48 us
  starting transfers between devices: 24.9 us -> 3.58 us
  matrix products: 13.8 us -> 0 us
  Pallas kernels: 0 us -> 9.75 us
  other arithmetic: 8.16 us -> 0 us
  waiting for transfers between devices: 11.5 us -> 5.3 us
    gather x202 -> x0, local copies, waits for them, and re-layouts: 110 us -> none
    another operation x12 -> x0, local copies, waits for them, and re-layouts: 60 us -> none  [the longest x6 57.4 us: toeplitz(): repeated = jnp.tile(padded, (1,) * len(leading) + (frame_size,))]
    all_gather x2 -> x0, blocking collectives: 39.1 us -> none  [the longest x1 22.2 us: shards(): group_scale = lax.all_gather(local_scale, 'tp', axis=0, tiled=True)]
    all_to_all x0 -> x2, blocking collectives: none -> 37.2 us  [the longest x1 23.4 us: shards(): lax.all_to_all(spread, 'tp', split_axis=0, concat_axis=0, tiled=True)]
    all_to_all x4 -> x1, starting transfers between devices: 24.9 us -> 3.58 us  [shards(): lax.all_to_all(picked, 'st', split_axis=0, concat_axis=0, tiled=True)]
    slice x12 -> x0, local copies, waits for them, and re-layouts: 21.2 us -> none  [the longest x3 11.2 us: correlate(): bands[..., step_index * frame_size:(step_index + 1) * frame_size]]
    dot_general x15 -> x0, matrix products: 13.8 us -> none  [correlate(): jnp.einsum('ncbp,ncip->ncbi', frames[:, :, step_index:step_index + blocks...]
    while x9 -> x0, local copies, waits for them, and re-layouts: 13.8 us -> none
  transfers between devices with their start and end apart: 4 -> 1, of which waited for: 2 -> 1; matrix products, arithmetic and copies ran while one was open for 3% -> 1% of each run, Pallas kernels for 0% -> 5%
where the time goes in v1:
time: 63.8 us; the launch traced here: 63.4 us
  blocking collectives  37.2 us (58%)
  Pallas kernels  9.75 us (15%)
  local copies, waits for them, and re-layouts  7.48 us (12%)
  waiting for transfers between devices  5.3 us (8%)
  starting transfers between devices  3.58 us (6%)
    all_to_all x1, blocking collectives, shards(): lax.all_to_all(spread, 'tp', split_axis=0, concat_axis=0, tiled=True)  23.4 us
    all_to_all x1, blocking collectives, shards(): asks = lax.all_to_all(asked, 'st', split_axis=0, concat_axis=0, tiled=True)  13.8 us
    unnamed x10, local copies, waits for them, and re-layouts  7.48 us
    all_to_all x1, waiting for transfers between devices, shards(): lax.all_to_all(picked, 'st', split_axis=0, concat_axis=0, tiled=True)  5.3 us
    all_to_all x1, starting transfers between devices, shards(): lax.all_to_all(picked, 'st', split_axis=0, concat_axis=0, tiled=True)  3.58 us
    pallas_call x1, Pallas kernels, shards(): pl.pallas_call(lambda *refs: build_bands(entries, *refs), out_shape=(jax....  3.29 us
    pallas_call x1, Pallas kernels, shards(): pl.pallas_call(lambda *refs: correlate(entries, *refs), out_shape=jax.Sha...  3.29 us
    pallas_call x1, Pallas kernels, shards(): pl.pallas_call(lambda *refs: pick(groups, *refs), out_shape=jax.ShapeDtyp...  1.64 us
  transfers between devices with their start and end apart: 1, of which 1 were waited for; matrix products, arithmetic and copies ran while one was open for 1% of the time, Pallas kernels for 5%

profile of v1, /device:TPU:1, one launch (start us, length us, event | category | flops | bytes accessed | tf_op | source)
XLA Modules:
  0.0 63.4 jit_solution(11219362762633996900)
XLA Ops:
  0.0 0.7 %copy.5.refs_1_ = bf16[2,3,1424]{2,1,0:T(4,128)(2,1)S(1)} copy(bf16[2,3,1424]{2,0,1:T(2,128)(2,1)} %param.4) | data formatting | bytes 34176 | tf_op args[0]
  0.7 0.0 copy-start.3
  0.7 0.7 %copy-done.3 = s32[2,12]{1,0:T(2,128)S(1)} copy-done((s32[2,12]{1,0:T(2,128)S(1)}, s32[2,12]{1,0:T(2,128)}, u32[]{:S(2)}) %copy-start.3) | copy-done | bytes 120
  1.4 1.5 %prepare.1 = (bf16[16,80,128]{2,1,0:T(8,128)(2,1)S(1)}, s32[16,1,128]{2,1,0:T(1,128)S(1)}, s32[1,128]{1,0:T(1,128)S(1)}) custom-call(s32[2,12]{1,0:T(2,128)S(1)} %copy-done.3, bf16[2,3,1424]{2,1,0:T(4,128)(2,1)S(1)} %copy.5.refs_1_), custom_call_target="tpu_custom_call" | custom-call | tf_op jit(solution)/shard_map/prepare/pallas_call | solution.py:181
  3.0 13.8 %all_to_all.15.refs_0_ = s32[16,1,128]{2,1,0:T(1,128)S(1)} all-to-all(s32[16,1,128]{2,1,0:T(1,128)S(1)} %get-tuple-element.12), channel_id=1, replica_groups=mesh['st'=16,'tp'=16] {'st'}, dimensions={0} | all-to-all | bytes 16384 | tf_op jit(solution)/shard_map/all_to_all | solution.py:197
  16.7 23.4 %all_to_all.16.refs_1_ = bf16[16,80,128]{2,1,0:T(8,128)(2,1)S(1)} all-to-all(bf16[16,80,128]{2,1,0:T(8,128)(2,1)S(1)} %get-tuple-element.13), channel_id=1, replica_groups=mesh['st'=16,'tp'=16] {'tp'}, dimensions={0} | all-to-all | bytes 655360 | tf_op jit(solution)/shard_map/all_to_all | solution.py:198
  40.2 1.6 %pick.1 = bf16[16,120,128]{2,1,0:T(8,128)(2,1)} custom-call(s32[16,1,128]{2,1,0:T(1,128)S(1)} %all_to_all.15.refs_0_, bf16[16,80,128]{2,1,0:T(8,128)(2,1)S(1)} %all_to_all.16.refs_1_), custom_call_target="tpu_custom_call" | custom-call | tf_op jit(solution)/shard_map/pick/pallas_call | solution.py:212
  41.8 3.6 %all-to-all-start.2 = ((bf16[16,120,128]{2,1,0:T(8,128)(2,1)}), bf16[16,120,128]{2,1,0:T(8,128)(2,1)S(1)}, u32[]{:S(2)}, u32[]{:S(2)}) async-start(bf16[16,120,128]{2,1,0:T(8,128)(2,1)} %pick.1), calls=%async_computation.2 | async-start | bytes 983040 | tf_op jit(solution)/shard_map/all_to_all | solution.py:221
  45.4 0.9 %copy.6 = bf16[2,12,3,400]{3,2,1,0:T(4,128)(2,1)S(1)} copy(bf16[2,12,3,400]{3,0,2,1:T(2,128)(2,1)} %param.5) | data formatting | bytes 115200 | tf_op args[1]
  46.3 3.3 %bands.1 = (bf16[3,1536,512]{2,1,0:T(8,128)(2,1)S(1)}, f32[24,3,128]{2,1,0:T(4,128)S(1)}, bf16[256,512]{1,0:T(8,128)(2,1)S(1)}) custom-call(bf16[24,3,400]{2,1,0:T(4,128)(2,1)S(1)} %bitcast.1), custom_call_target="tpu_custom_call" | custom-call | tf_op jit(solution)/shard_map/bands/pallas_call | solution.py:199
  49.6 0.0 copy-start
  49.7 2.1 %copy-done = bf16[3,1536,512]{2,1,0:T(8,128)(2,1)} copy-done((bf16[3,1536,512]{2,1,0:T(8,128)(2,1)}, bf16[3,1536,512]{2,1,0:T(8,128)(2,1)S(1)}, u32[]{:S(2)}) %copy-start) | copy-done | bytes 4718616
  51.8 5.3 %all-to-all-done.2.refs_2_ = bf16[16,120,128]{2,1,0:T(8,128)(2,1)S(1)} async-done(((bf16[16,120,128]{2,1,0:T(8,128)(2,1)}), bf16[16,120,128]{2,1,0:T(8,128)(2,1)S(1)}, u32[]{:S(2)}, u32[]{:S(2)}) %all-to-all-start.2) | async-done | bytes 491552 | tf_op jit(solution)/shard_map/all_to_all | solution.py:221
  57.1 0.0 copy-start.1
  57.1 2.3 %copy-done.1 = bf16[3,1536,512]{2,1,0:T(8,128)(2,1)S(1)} copy-done((bf16[3,1536,512]{2,1,0:T(8,128)(2,1)S(1)}, bf16[3,1536,512]{2,1,0:T(8,128)(2,1)}, u32[]{:S(2)}) %copy-start.1) | copy-done | bytes 4718616
  59.4 0.0 copy-start.2
  59.4 0.7 %copy-done.2 = s32[2,12]{1,0:T(2,128)S(1)} copy-done((s32[2,12]{1,0:T(2,128)S(1)}, s32[2,12]{1,0:T(2,128)}, u32[]{:S(2)}) %copy-start.2) | copy-done | bytes 120
  60.1 3.3 %correlate.1 = f32[2,768]{1,0:T(2,128)} custom-call(s32[1,128]{1,0:T(1,128)S(1)} %get-tuple-element.11.refs_0_, s32[2,12]{1,0:T(2,128)S(1)} %copy-done.2, bf16[16,120,128]{2,1,0:T(8,128)(2,1)S(1)} %all-to-all-done.2.refs_2_, bf16[3,1536,512]{2,1,0:T(8,128)(2,1)S(1)} %copy-done.1, f32[24,3,128]{2,1,0:T(4,128)S(1)} %get-tuple-element.15.refs_4_, ...), custom_call_target="tpu_custom_call" | custom-call | tf_op jit(solution)/shard_map/correlate/pallas_call | solution.py:222
Async XLA Ops:
  0.7 0.7 %copy-start.3 = (s32[2,12]{1,0:T(2,128)S(1)}, s32[2,12]{1,0:T(2,128)}, u32[]{:S(2)}) copy-start(s32[2,12]{1,0:T(2,128)} %refs_0_.1) | copy-start | bytes 292
  41.8 15.3 %all-to-all-start.2 = ((bf16[16,120,128]{2,1,0:T(8,128)(2,1)}), bf16[16,120,128]{2,1,0:T(8,128)(2,1)S(1)}, u32[]{:S(2)}, u32[]{:S(2)}) async-start(bf16[16,120,128]{2,1,0:T(8,128)(2,1)} %pick.1), calls=%async_computation.2 | async-start | bytes 983040 | tf_op jit(solution)/shard_map/all_to_all | solution.py:221
  49.6 2.1 %copy-start = (bf16[3,1536,512]{2,1,0:T(8,128)(2,1)}, bf16[3,1536,512]{2,1,0:T(8,128)(2,1)S(1)}, u32[]{:S(2)}) copy-start(bf16[3,1536,512]{2,1,0:T(8,128)(2,1)S(1)} %get-tuple-element.14.refs_3_) | copy-start | bytes 14155780
  57.1 2.3 %copy-start.1 = (bf16[3,1536,512]{2,1,0:T(8,128)(2,1)S(1)}, bf16[3,1536,512]{2,1,0:T(8,128)(2,1)}, u32[]{:S(2)}) copy-start(bf16[3,1536,512]{2,1,0:T(8,128)(2,1)} %copy-done) | copy-start | bytes 14155780
  59.4 0.7 %copy-start.2 = (s32[2,12]{1,0:T(2,128)S(1)}, s32[2,12]{1,0:T(2,128)}, u32[]{:S(2)}) copy-start(s32[2,12]{1,0:T(2,128)} %refs_1_.2) | copy-start | bytes 292

commit v2 on v1

--- a/solution.py
+++ b/solution.py
@@ -19,14 +19,17 @@
 BLOCKS = WIN // LANES
 
 
-def prepare(groups, entries, station_ref, data_ref, out_ref, ask_ref, slot_ref, scratch, count):
+def prepare(
+    groups, entries, station_ref, shift_ref, data_ref, out_ref, ask_ref, slot_ref, scratch, count
+):
     list_size = station_ref.shape[1]
+    owned = data_ref.shape[1]
     scratch[...] = jnp.zeros_like(scratch)
-    for k in range(data_ref.shape[0]):
-        x = data_ref[k].astype(jnp.float32)
+    for c in range(CH):
+        x = data_ref[c].astype(jnp.float32)
         for q in range(TILES):
             width = min(LANES, DLEN - q * LANES)
-            scratch[pl.ds(k * ROWS + q, CH, stride=TILES), 0:width] = x[
+            scratch[pl.ds(c * TILES + q, owned, stride=ROWS), 0:width] = x[
                 :, q * LANES : q * LANES + width
             ]
     packed = scratch[...].astype(jnp.bfloat16)
@@ -35,32 +38,38 @@
     for g in range(groups):
         count[g] = 0
         for s in range(CAP):
-            ask_ref[g, 0, s] = 0
+            ask_ref[0, g * CAP + s] = 0
     for e in range(entries):
         station = station_ref[e // list_size, e % list_size]
         g = station // 32
         position = jnp.minimum(count[g], CAP - 1)
         count[g] = position + 1
-        ask_ref[g, 0, position] = station - g * 32
+        ask_ref[0, g * CAP + position] = station - g * 32
         slot_ref[0, e] = g * CAP + position
+        slot_ref[1, e] = shift_ref[e // list_size, e % list_size]
 
 
 def build_bands(entries, templates_ref, band_ref, scale_ref, ones_ref, scratch):
     scratch[...] = jnp.zeros_like(scratch)
 
-    def step(e, carry):
-        x = templates_ref[e].astype(jnp.float32)
-        scratch[0:CH, 0:TLEN] = x
-        energy = jnp.sum(x * x, axis=1, keepdims=True)
-        scale = lax.rsqrt(energy / TLEN + EPS) / TLEN
-        scale_ref[e] = jnp.broadcast_to(scale, (CH, LANES))
+    list_size = templates_ref.shape[0]
+    owned = templates_ref.shape[2]
+
+    def step(k, carry):
         for c in range(CH):
-            rows = jnp.broadcast_to(scratch[c : c + 1, :], (HALF, DEPTH))
-            band = pltpu.roll(rows, 0, 1, stride=1, stride_axis=0)
-            band_ref[c, pl.ds(pl.multiple_of(e * HALF, HALF), HALF), :] = band.astype(jnp.bfloat16)
+            x = templates_ref[k, c].astype(jnp.float32)
+            scratch[0:owned, 0:TLEN] = x
+            energy = jnp.sum(x * x, axis=1, keepdims=True)
+            scale = lax.rsqrt(energy / TLEN + EPS) / TLEN
+            scale_ref[k, c] = jnp.broadcast_to(scale, (owned, LANES))
+            for t in range(owned):
+                rows = jnp.broadcast_to(scratch[t : t + 1, :], (HALF, DEPTH))
+                band = pltpu.roll(rows, 0, 1, stride=1, stride_axis=0)
+                place = pl.multiple_of((t * list_size + k) * HALF, HALF)
+                band_ref[c, pl.ds(place, HALF), :] = band.astype(jnp.bfloat16)
         return carry
 
-    lax.fori_loop(0, entries, step, 0)
+    lax.fori_loop(0, list_size, step, 0)
     r = lax.broadcasted_iota(jnp.int32, (LANES, LANES), 0)
     i = lax.broadcasted_iota(jnp.int32, (LANES, LANES), 1)
     kinds = (r >= i, r >= 0, r - i < TLEN - 384, r - i < TLEN - 512)
@@ -71,9 +80,10 @@
 
 
 def pick(groups, ask_ref, data_ref, out_ref, sem):
+    me = lax.axis_index("st")
     for i in range(groups):
         for s in range(CAP):
-            station = ask_ref[i, 0, s]
+            station = ask_ref[i, 0, me * CAP + s]
             t = station // 2
             k = station - t * 2
             pltpu.make_async_copy(
@@ -85,7 +95,7 @@
 
 
 def correlate(
-    entries, slot_ref, shift_ref, data_ref, band_ref, scale_ref, ones_ref, out_ref,
+    entries, slot_ref, data_ref, band_ref, scale_ref, ones_ref, out_ref,
     wide, shifted, squares, sums,
 ):
     groups, rows, _ = data_ref.shape
@@ -96,7 +106,7 @@
     lane = lax.broadcasted_iota(jnp.int32, (ROWS, LANES), 1)
     lane8 = lax.broadcasted_iota(jnp.int32, (8, LANES), 1)
     for e in range(entries):
-        shift = shift_ref[e // list_size, e % list_size]
+        shift = slot_ref[1, e]
         base = slot_ref[0, e] * ROWS
         for h in range(2):
             moved = shift + h * HALF
@@ -157,8 +167,8 @@
                     + sums[start + 4 : start + 12, 3 * LANES :]
                 )
                 level = lax.rsqrt(energy / TLEN + EPS)
-                totals[e // list_size] = totals[e // list_size] + raw * level * scale_ref[e][
-                    c : c + 1, :
+                totals[e // list_size] = totals[e // list_size] + raw * level * scale_ref[
+                    e % list_size, c, e // list_size : e // list_size + 1, :
                 ]
     for t, total in enumerate(totals):
         for b in range(BLOCKS):
@@ -175,54 +185,54 @@
     vmem = pl.BlockSpec(memory_space=pltpu.VMEM)
     anywhere = pl.BlockSpec(memory_space=pl.ANY)
 
-    def params():
-        return pltpu.CompilerParams(vmem_limit_bytes=48 * 2**20)
+    def params(mebibytes):
+        return pltpu.CompilerParams(vmem_limit_bytes=mebibytes * 2**20)
 
     spread, asked, slots = pl.pallas_call(
         lambda *refs: prepare(groups, entries, *refs),
         out_shape=(
             jax.ShapeDtypeStruct((peers, owned * ROWS, LANES), jnp.bfloat16),
-            jax.ShapeDtypeStruct((groups, 1, LANES), jnp.int32),
             jax.ShapeDtypeStruct((1, LANES), jnp.int32),
+            jax.ShapeDtypeStruct((2, LANES), jnp.int32),
         ),
-        in_specs=[smem, vmem],
+        in_specs=[smem, smem, vmem],
         out_specs=(vmem, smem, smem),
         scratch_shapes=[
             pltpu.VMEM((owned * ROWS, LANES), jnp.float32),
             pltpu.SMEM((groups,), jnp.int32),
         ],
-        compiler_params=params(),
+        compiler_params=params(4),
         name="prepare",
-    )(station_list, continuous)
-    asks = lax.all_to_all(asked, "st", split_axis=0, concat_axis=0, tiled=True)
+    )(station_list, moveouts, jnp.swapaxes(continuous, 0, 1))
+    asks = lax.all_gather(asked, "st", axis=0, tiled=False)
     group_rows = lax.all_to_all(spread, "tp", split_axis=0, concat_axis=0, tiled=True)
     bands, scales, ones = pl.pallas_call(
         lambda *refs: build_bands(entries, *refs),
         out_shape=(
             jax.ShapeDtypeStruct((CH, entries * HALF, DEPTH), jnp.bfloat16),
-            jax.ShapeDtypeStruct((entries, CH, LANES), jnp.float32),
+            jax.ShapeDtypeStruct((list_size, CH, template_count, LANES), jnp.float32),
             jax.ShapeDtypeStruct((2 * LANES, 4 * LANES), jnp.bfloat16),
         ),
         in_specs=[vmem],
         out_specs=(vmem, vmem, vmem),
         scratch_shapes=[pltpu.VMEM((8, DEPTH), jnp.float32)],
-        compiler_params=params(),
+        compiler_params=params(12),
         name="bands",
-    )(templates.reshape(entries, CH, TLEN))
+    )(jnp.transpose(templates, (1, 2, 0, 3)))
     picked = pl.pallas_call(
         lambda *refs: pick(groups, *refs),
         out_shape=jax.ShapeDtypeStruct((groups, CAP * ROWS, LANES), jnp.bfloat16),
         in_specs=[smem, anywhere],
         out_specs=anywhere,
         scratch_shapes=[pltpu.SemaphoreType.DMA],
-        compiler_params=params(),
+        compiler_params=params(2),
         name="pick",
     )(asks, group_rows)
     records = lax.all_to_all(picked, "st", split_axis=0, concat_axis=0, tiled=True)
     return pl.pallas_call(
         lambda *refs: correlate(entries, *refs),
         out_shape=jax.ShapeDtypeStruct((template_count, WIN), jnp.float32),
-        in_specs=[smem, smem, vmem, vmem, vmem, vmem],
+        in_specs=[smem, vmem, vmem, vmem, vmem],
         out_specs=vmem,
         scratch_shapes=[
             pltpu.VMEM((groups * CAP * ROWS + 8, LANES), jnp.float32),
@@ -230,9 +240,9 @@
             pltpu.VMEM((entries * ROWS, 2 * LANES), jnp.bfloat16),
             pltpu.VMEM((entries * ROWS, 4 * LANES), jnp.float32),
         ],
-        compiler_params=params(),
+        compiler_params=params(16),
         name="correlate",
-    )(slots, moveouts, records, bands, scales, ones)
+    )(slots, records, bands, scales, ones)
 
 
 def solution(mesh):

time: 63.8 us -> 56.1 us (0.88)
  the two profiles are of different devices: /device:TPU:1 before, /device:TPU:32 now
where the time goes in v2:
time: 56.1 us; the launch traced here: 55.6 us
  blocking collectives  20.9 us (37%)
  starting transfers between devices  13.8 us (25%)
  Pallas kernels  9.12 us (16%)
  local copies, waits for them, and re-layouts  7.43 us (13%)
  waiting for transfers between devices  4.29 us (8%)
    all_gather x1, blocking collectives, shards(): asks = lax.all_gather(asked, 'st', axis=0, tiled=False)  20.9 us
    all_to_all x1, starting transfers between devices, shards(): lax.all_to_all(spread, 'tp', split_axis=0, concat_axis=0, tiled=True)  8.6 us
    unnamed x12, local copies, waits for them, and re-layouts  7.43 us
    all_to_all x1, starting transfers between devices, shards(): lax.all_to_all(picked, 'st', split_axis=0, concat_axis=0, tiled=True)  5.22 us
    all_to_all x1, waiting for transfers between devices, shards(): lax.all_to_all(picked, 'st', split_axis=0, concat_axis=0, tiled=True)  4.28 us
    pallas_call x1, Pallas kernels, shards(): pl.pallas_call(lambda *refs: correlate(entries, *refs), out_shape=jax.Sha...  3.28 us
    pallas_call x1, Pallas kernels, shards(): pl.pallas_call(lambda *refs: build_bands(entries, *refs), out_shape=(jax....  2.65 us
    pallas_call x1, Pallas kernels, shards(): pl.pallas_call(lambda *refs: pick(groups, *refs), out_shape=jax.ShapeDtyp...  1.67 us
  transfers between devices with their start and end apart: 2, of which 1 were waited for; matrix products, arithmetic and copies ran while one was open for 0% of the time, Pallas kernels for 5%

profile of v2, /device:TPU:32, one launch (start us, length us, event | category | flops | bytes accessed | tf_op | source)
XLA Modules:
  0.0 55.6 jit_solution(976098271281137569)
XLA Ops:
  0.0 0.0 copy-start.3
  0.0 0.7 %copy-done.3 = bf16[2,3,1424]{2,0,1:T(2,128)(2,1)S(1)} copy-done((bf16[2,3,1424]{2,0,1:T(2,128)(2,1)S(1)}, bf16[2,3,1424]{2,0,1:T(2,128)(2,1)}, u32[]{:S(2)}) %copy-start.3) | copy-done | bytes 17112
  0.7 0.0 copy-start.4
  0.7 0.7 %copy-done.4 = s32[2,12]{1,0:T(2,128)S(1)} copy-done((s32[2,12]{1,0:T(2,128)S(1)}, s32[2,12]{1,0:T(2,128)}, u32[]{:S(2)}) %copy-start.4) | copy-done | bytes 120
  1.4 0.0 copy-start.5
  1.4 0.7 %copy-done.5 = s32[2,12]{1,0:T(2,128)S(1)} copy-done((s32[2,12]{1,0:T(2,128)S(1)}, s32[2,12]{1,0:T(2,128)}, u32[]{:S(2)}) %copy-start.5) | copy-done | bytes 120
  2.1 1.5 %prepare.1 = (bf16[16,80,128]{2,1,0:T(8,128)(2,1)}, s32[1,128]{1,0:T(1,128)S(1)}, s32[2,128]{1,0:T(2,128)S(1)}) custom-call(s32[2,12]{1,0:T(2,128)S(1)} %copy-done.4, s32[2,12]{1,0:T(2,128)S(1)} %copy-done.5, bf16[3,2,1424]{2,1,0:T(2,128)(2,1)S(1)} %bitcast.4), custom_call_target="tpu_custom_call" | custom-call | tf_op jit(solution)/shard_map/prepare/pallas_call | solution.py:191
  3.6 8.6 %all-to-all-start = ((bf16[16,80,128]{2,1,0:T(8,128)(2,1)}), bf16[16,80,128]{2,1,0:T(8,128)(2,1)S(1)}, u32[]{:S(2)}, u32[]{:S(2)}) async-start(bf16[16,80,128]{2,1,0:T(8,128)(2,1)} %get-tuple-element.13), calls=%async_computation | async-start | bytes 655360 | tf_op jit(solution)/shard_map/all_to_all | solution.py:208
  12.2 20.9 %all-gather.1.refs_0_ = s32[16,1,128]{2,1,0:T(1,128)S(1)} all-gather(s32[1,1,128]{2,1,0:T(1,128)S(1)} %bitcast.5), channel_id=2, replica_groups=mesh['st'=16,'tp'=16] {'st'}, dimensions={0}, use_global_device_ids=true | all-gather | bytes 8704 | tf_op jit(solution)/shard_map/all_gather | solution.py:207
  33.1 0.0 all-to-all-done.refs_1_
  33.1 1.7 %pick.1 = bf16[16,120,128]{2,1,0:T(8,128)(2,1)} custom-call(s32[16,1,128]{2,1,0:T(1,128)S(1)} %all-gather.1.refs_0_, bf16[16,80,128]{2,1,0:T(8,128)(2,1)S(1)} %all-to-all-done.refs_1_), custom_call_target="tpu_custom_call" | custom-call | tf_op jit(solution)/shard_map/pick/pallas_call | solution.py:222
  34.8 5.2 %all-to-all-start.1 = ((bf16[16,120,128]{2,1,0:T(8,128)(2,1)}), bf16[16,120,128]{2,1,0:T(8,128)(2,1)S(1)}, u32[]{:S(2)}, u32[]{:S(2)}) async-start(bf16[16,120,128]{2,1,0:T(8,128)(2,1)} %pick.1), calls=%async_computation.1 | async-start | bytes 983040 | tf_op jit(solution)/shard_map/all_to_all | solution.py:231
  40.0 0.0 copy-start.2
  40.0 0.9 %copy-done.2 = bf16[2,12,3,400]{3,0,2,1:T(2,128)(2,1)S(1)} copy-done((bf16[2,12,3,400]{3,0,2,1:T(2,128)(2,1)S(1)}, bf16[2,12,3,400]{3,0,2,1:T(2,128)(2,1)}, u32[]{:S(2)}) %copy-start.2) | copy-done | bytes 57624
  40.9 2.6 %bands.1 = (bf16[3,1536,512]{2,1,0:T(8,128)(2,1)S(1)}, f32[12,3,2,128]{3,2,1,0:T(2,128)S(1)}, bf16[256,512]{1,0:T(8,128)(2,1)S(1)}) custom-call(bf16[12,3,2,400]{3,2,1,0:T(2,128)(2,1)S(1)} %bitcast.3), custom_call_target="tpu_custom_call" | custom-call | tf_op jit(solution)/shard_map/bands/pallas_call | solution.py:209
  43.6 0.0 copy-start
  43.6 2.1 %copy-done = bf16[3,1536,512]{2,1,0:T(8,128)(2,1)} copy-done((bf16[3,1536,512]{2,1,0:T(8,128)(2,1)}, bf16[3,1536,512]{2,1,0:T(8,128)(2,1)S(1)}, u32[]{:S(2)}) %copy-start) | copy-done | bytes 4718616
  45.7 4.3 %all-to-all-done.1.refs_1_ = bf16[16,120,128]{2,1,0:T(8,128)(2,1)S(1)} async-done(((bf16[16,120,128]{2,1,0:T(8,128)(2,1)}), bf16[16,120,128]{2,1,0:T(8,128)(2,1)S(1)}, u32[]{:S(2)}, u32[]{:S(2)}) %all-to-all-start.1) | async-done | bytes 491552 | tf_op jit(solution)/shard_map/all_to_all | solution.py:231
  50.0 0.0 copy-start.1
  50.0 2.3 %copy-done.1 = bf16[3,1536,512]{2,1,0:T(8,128)(2,1)S(1)} copy-done((bf16[3,1536,512]{2,1,0:T(8,128)(2,1)S(1)}, bf16[3,1536,512]{2,1,0:T(8,128)(2,1)}, u32[]{:S(2)}) %copy-start.1) | copy-done | bytes 4718616
  52.3 3.3 %correlate.1 = f32[2,768]{1,0:T(2,128)} custom-call(s32[2,128]{1,0:T(2,128)S(1)} %get-tuple-element.11.refs_0_, bf16[16,120,128]{2,1,0:T(8,128)(2,1)S(1)} %all-to-all-done.1.refs_1_, bf16[3,1536,512]{2,1,0:T(8,128)(2,1)S(1)} %copy-done.1, f32[12,3,2,128]{3,2,1,0:T(2,128)S(1)} %get-tuple-element.15.refs_3_, bf16[256,512]{1,0:T(8,128)(2,1)S(1)} %get-tuple-element.16.refs_4_), custom_call_target="tpu_custom_call" | custom-call | tf_op jit(solution)/shard_map/correlate/pallas_call | solution.py:232
Async XLA Ops:
  0.0 0.7 %copy-start.3 = (bf16[2,3,1424]{2,0,1:T(2,128)(2,1)S(1)}, bf16[2,3,1424]{2,0,1:T(2,128)(2,1)}, u32[]{:S(2)}) copy-start(bf16[2,3,1424]{2,0,1:T(2,128)(2,1)} %param.4) | copy-start | bytes 51268
  0.7 0.7 %copy-start.4 = (s32[2,12]{1,0:T(2,128)S(1)}, s32[2,12]{1,0:T(2,128)}, u32[]{:S(2)}) copy-start(s32[2,12]{1,0:T(2,128)} %refs_0_.1) | copy-start | bytes 292
  1.4 0.7 %copy-start.5 = (s32[2,12]{1,0:T(2,128)S(1)}, s32[2,12]{1,0:T(2,128)}, u32[]{:S(2)}) copy-start(s32[2,12]{1,0:T(2,128)} %refs_1_.1) | copy-start | bytes 292
  3.6 29.5 %all-to-all-start = ((bf16[16,80,128]{2,1,0:T(8,128)(2,1)}), bf16[16,80,128]{2,1,0:T(8,128)(2,1)S(1)}, u32[]{:S(2)}, u32[]{:S(2)}) async-start(bf16[16,80,128]{2,1,0:T(8,128)(2,1)} %get-tuple-element.13), calls=%async_computation | async-start | bytes 655360 | tf_op jit(solution)/shard_map/all_to_all | solution.py:208
  34.8 15.2 %all-to-all-start.1 = ((bf16[16,120,128]{2,1,0:T(8,128)(2,1)}), bf16[16,120,128]{2,1,0:T(8,128)(2,1)S(1)}, u32[]{:S(2)}, u32[]{:S(2)}) async-start(bf16[16,120,128]{2,1,0:T(8,128)(2,1)} %pick.1), calls=%async_computation.1 | async-start | bytes 983040 | tf_op jit(solution)/shard_map/all_to_all | solution.py:231
  40.0 0.9 %copy-start.2 = (bf16[2,12,3,400]{3,0,2,1:T(2,128)(2,1)S(1)}, bf16[2,12,3,400]{3,0,2,1:T(2,128)(2,1)}, u32[]{:S(2)}) copy-start(bf16[2,12,3,400]{3,0,2,1:T(2,128)(2,1)} %param.5) | copy-start | bytes 172804
  43.6 2.1 %copy-start = (bf16[3,1536,512]{2,1,0:T(8,128)(2,1)}, bf16[3,1536,512]{2,1,0:T(8,128)(2,1)S(1)}, u32[]{:S(2)}) copy-start(bf16[3,1536,512]{2,1,0:T(8,128)(2,1)S(1)} %get-tuple-element.14.refs_2_) | copy-start | bytes 14155780
  50.0 2.3 %copy-start.1 = (bf16[3,1536,512]{2,1,0:T(8,128)(2,1)S(1)}, bf16[3,1536,512]{2,1,0:T(8,128)(2,1)}, u32[]{:S(2)}) copy-start(bf16[3,1536,512]{2,1,0:T(8,128)(2,1)} %copy-done) | copy-start | bytes 14155780

commit v3 on v2

--- a/solution.py
+++ b/solution.py
@@ -17,6 +17,15 @@
 HALF = 64
 DEPTH = 512
 BLOCKS = WIN // LANES
+SIDE = 4
+
+
+def rotation(dy, dx):
+    return [
+        (y * SIDE + x, (y + dy) % SIDE * SIDE + (x + dx) % SIDE)
+        for y in range(SIDE)
+        for x in range(SIDE)
+    ]
 
 
 def prepare(
@@ -49,7 +58,7 @@
         slot_ref[1, e] = shift_ref[e // list_size, e % list_size]
 
 
-def build_bands(entries, templates_ref, band_ref, scale_ref, ones_ref, scratch):
+def build_bands(templates_ref, band_out, scale_ref, ones_ref, scratch, band_ref, sem):
     scratch[...] = jnp.zeros_like(scratch)
 
     list_size = templates_ref.shape[0]
@@ -67,6 +76,9 @@
                 band = pltpu.roll(rows, 0, 1, stride=1, stride_axis=0)
                 place = pl.multiple_of((t * list_size + k) * HALF, HALF)
                 band_ref[c, pl.ds(place, HALF), :] = band.astype(jnp.bfloat16)
+                pltpu.make_async_copy(
+                    band_ref.at[c, pl.ds(place, HALF)], band_out.at[c, pl.ds(place, HALF)], sem
+                ).start()
         return carry
 
     lax.fori_loop(0, list_size, step, 0)
@@ -77,27 +89,47 @@
         block = jnp.where(kind, 1.0, 0.0).astype(jnp.bfloat16)
         ones_ref[0:LANES, n * LANES : (n + 1) * LANES] = block
         ones_ref[LANES : 2 * LANES, n * LANES : (n + 1) * LANES] = block
-
-
-def pick(groups, ask_ref, data_ref, out_ref, sem):
+    pltpu.make_async_copy(band_ref, band_out, sem).wait()
+
+
+def pick(*refs):
+    asks, (data_ref, out_ref, sem) = refs[:SIDE], refs[SIDE:]
     me = lax.axis_index("st")
-    for i in range(groups):
-        for s in range(CAP):
-            station = ask_ref[i, 0, me * CAP + s]
-            t = station // 2
-            k = station - t * 2
+    y, x = me // SIDE, me % SIDE
+    for dy in range(SIDE):
+        for dx in range(SIDE):
+            i = ((y + SIDE - dy) % SIDE) * SIDE + (x + SIDE - dx) % SIDE
+            for s in range(CAP):
+                station = asks[dy][dx, me * CAP + s]
+                t = station // 2
+                k = station - t * 2
+                pltpu.make_async_copy(
+                    data_ref.at[t, pl.ds(pl.multiple_of(k * ROWS, 8), ROWS)],
+                    out_ref.at[i, pl.ds(s * ROWS, ROWS)],
+                    sem,
+                ).start()
+    pltpu.make_async_copy(out_ref, out_ref, sem).wait()
+
+
+def correlate(
+    entries, slot_ref, data_ref, band_in, scale_ref, ones_ref, out_ref,
+    wide, shifted, squares, sums, band_ref, sems,
+):
+    quads = entries // 4
+    loads = []
+    for quad in range(quads):
+        part = pl.ds(quad * 4 * HALF, 4 * HALF)
+        loads.append(
             pltpu.make_async_copy(
-                data_ref.at[t, pl.ds(pl.multiple_of(k * ROWS, 8), ROWS)],
-                out_ref.at[i, pl.ds(s * ROWS, ROWS)],
-                sem,
-            ).start()
-    pltpu.make_async_copy(out_ref, out_ref, sem).wait()
-
-
-def correlate(
-    entries, slot_ref, data_ref, band_ref, scale_ref, ones_ref, out_ref,
-    wide, shifted, squares, sums,
-):
+                band_in.at[:, part], band_ref.at[:, part], sems.at[quad]
+            )
+        )
+        for c in range(CH):
+            for n in range(1):
+                part = pl.ds(quad * 4 * HALF + n * (4 * HALF // 1), 4 * HALF // 1)
+                pltpu.make_async_copy(
+                    band_in.at[c, part], band_ref.at[c, part], sems.at[quad]
+                ).start()
     groups, rows, _ = data_ref.shape
     list_size = entries // out_ref.shape[0]
     for g in range(groups):
@@ -126,7 +158,8 @@
                 ).astype(jnp.bfloat16)
     sums[...] = jnp.dot(squares[...], ones_ref[...], preferred_element_type=jnp.float32)
     totals = [jnp.zeros((8, LANES), jnp.float32) for _ in range(out_ref.shape[0])]
-    for quad in range(entries // 4):
+    for quad in range(quads):
+        loads[quad].wait()
         for c in range(CH):
             frames = []
             for n in range(4):
@@ -184,6 +217,10 @@
     smem = pl.BlockSpec(memory_space=pltpu.SMEM)
     vmem = pl.BlockSpec(memory_space=pltpu.VMEM)
     anywhere = pl.BlockSpec(memory_space=pl.ANY)
+    hbm = pl.BlockSpec(memory_space=pltpu.HBM)
+
+    def from_hbm(array):
+        return pltpu.with_memory_space_constraint(array, pltpu.HBM)
 
     def params(mebibytes):
         return pltpu.CompilerParams(vmem_limit_bytes=mebibytes * 2**20)
@@ -203,46 +240,54 @@
         ],
         compiler_params=params(4),
         name="prepare",
-    )(station_list, moveouts, jnp.swapaxes(continuous, 0, 1))
-    asks = lax.all_gather(asked, "st", axis=0, tiled=False)
+    )(from_hbm(station_list), from_hbm(moveouts), from_hbm(jnp.swapaxes(continuous, 0, 1)))
+    along_x = [asked] + [lax.ppermute(asked, "st", rotation(0, d)) for d in range(1, SIDE)]
+    row = jnp.concatenate(along_x, axis=0)
+    asks = [row] + [lax.ppermute(row, "st", rotation(d, 0)) for d in range(1, SIDE)]
     group_rows = lax.all_to_all(spread, "tp", split_axis=0, concat_axis=0, tiled=True)
     bands, scales, ones = pl.pallas_call(
-        lambda *refs: build_bands(entries, *refs),
+        build_bands,
         out_shape=(
-            jax.ShapeDtypeStruct((CH, entries * HALF, DEPTH), jnp.bfloat16),
+            pltpu.HBM((CH, entries * HALF, DEPTH), jnp.bfloat16),
             jax.ShapeDtypeStruct((list_size, CH, template_count, LANES), jnp.float32),
             jax.ShapeDtypeStruct((2 * LANES, 4 * LANES), jnp.bfloat16),
         ),
         in_specs=[vmem],
-        out_specs=(vmem, vmem, vmem),
-        scratch_shapes=[pltpu.VMEM((8, DEPTH), jnp.float32)],
+        out_specs=(hbm, vmem, vmem),
+        scratch_shapes=[
+            pltpu.VMEM((8, DEPTH), jnp.float32),
+            pltpu.VMEM((CH, entries * HALF, DEPTH), jnp.bfloat16),
+            pltpu.SemaphoreType.DMA,
+        ],
         compiler_params=params(12),
         name="bands",
-    )(jnp.transpose(templates, (1, 2, 0, 3)))
+    )(from_hbm(jnp.transpose(templates, (1, 2, 0, 3))))
     picked = pl.pallas_call(
-        lambda *refs: pick(groups, *refs),
+        pick,
         out_shape=jax.ShapeDtypeStruct((groups, CAP * ROWS, LANES), jnp.bfloat16),
-        in_specs=[smem, anywhere],
+        in_specs=[smem] * SIDE + [anywhere],
         out_specs=anywhere,
         scratch_shapes=[pltpu.SemaphoreType.DMA],
         compiler_params=params(2),
         name="pick",
-    )(asks, group_rows)
+    )(*asks, group_rows)
     records = lax.all_to_all(picked, "st", split_axis=0, concat_axis=0, tiled=True)
     return pl.pallas_call(
         lambda *refs: correlate(entries, *refs),
         out_shape=jax.ShapeDtypeStruct((template_count, WIN), jnp.float32),
-        in_specs=[smem, vmem, vmem, vmem, vmem],
+        in_specs=[smem, vmem, hbm, vmem, vmem],
         out_specs=vmem,
         scratch_shapes=[
             pltpu.VMEM((groups * CAP * ROWS + 8, LANES), jnp.float32),
             pltpu.VMEM((2, entries * ROWS, LANES), jnp.float32),
             pltpu.VMEM((entries * ROWS, 2 * LANES), jnp.bfloat16),
             pltpu.VMEM((entries * ROWS, 4 * LANES), jnp.float32),
+            pltpu.VMEM((CH, entries * HALF, DEPTH), jnp.bfloat16),
+            pltpu.SemaphoreType.DMA((entries // 4,)),
         ],
         compiler_params=params(16),
         name="correlate",
-    )(slots, records, bands, scales, ones)
+    )(slots, records, from_hbm(bands), scales, ones)
 
 
 def solution(mesh):

time: 56.1 us -> 49.6 us (0.88)
  the two profiles are of different devices: /device:TPU:32 before, /device:TPU:1 now
where the time goes in v3:
time: 49.6 us; the launch traced here: 49.2 us
  starting transfers between devices  23.6 us (48%)
  Pallas kernels  13.5 us (27%)
  waiting for transfers between devices  12.1 us (24%)
    all_to_all x1, starting transfers between devices, shards(): lax.all_to_all(spread, 'tp', split_axis=0, concat_axis=0, tiled=True)  9.99 us
    all_to_all x1, starting transfers between devices, shards(): lax.all_to_all(picked, 'st', split_axis=0, concat_axis=0, tiled=True)  6.11 us
    pallas_call x1, Pallas kernels, shards(): pl.pallas_call(lambda *refs: correlate(entries, *refs), out_shape=jax.Sha...  5.95 us
    all_to_all x1, waiting for transfers between devices, shards(): lax.all_to_all(picked, 'st', split_axis=0, concat_axis=0, tiled=True)  5.88 us
    pallas_call x1, Pallas kernels, shards(): pl.pallas_call(build_bands, out_shape=(pltpu.HBM((CH, entries * HALF, DEP...  4.15 us
    ppermute x3, starting transfers between devices, shards(): lax.ppermute(row, 'st', rotation(d, 0))  3.85 us
    ppermute x3, starting transfers between devices, shards(): lax.ppermute(asked, 'st', rotation(0, d))  3.6 us
    ppermute x3, waiting for transfers between devices, shards(): lax.ppermute(asked, 'st', rotation(0, d))  3.29 us
  transfers between devices with their start and end apart: 8, of which 5 were waited for; matrix products, arithmetic and copies ran while one was open for 0% of the time, Pallas kernels for 8%

profile of v3, /device:TPU:1, one launch (start us, length us, event | category | flops | bytes accessed | tf_op | source)
XLA Modules:
  0.0 49.2 jit_solution(16799377417420702347)
XLA Ops:
  0.0 1.7 %prepare.1 = (bf16[16,80,128]{2,1,0:T(8,128)(2,1)}, s32[1,128]{1,0:T(1,128)S(1)}, s32[2,128]{1,0:T(2,128)S(1)}) custom-call(s32[2,12]{1,0:T(2,128)} %refs_0_.1, s32[2,12]{1,0:T(2,128)} %refs_1_.1, bf16[3,2,1424]{2,1,0:T(2,128)(2,1)} %bitcast.3), custom_call_target="tpu_custom_call" | custom-call | tf_op jit(solution)/shard_map/prepare/pallas_call | solution.py:228
  1.7 10.0 %all-to-all-start = ((bf16[16,80,128]{2,1,0:T(8,128)(2,1)}), bf16[16,80,128]{2,1,0:T(8,128)(2,1)S(1)}, u32[]{:S(2)}, u32[]{:S(2)}) async-start(bf16[16,80,128]{2,1,0:T(8,128)(2,1)} %get-tuple-element.13), calls=%async_computation | async-start | bytes 655360 | tf_op jit(solution)/shard_map/all_to_all | solution.py:247
  11.7 2.5 %collective-permute-start.2 = (s32[1,128]{1,0:T(1,128)S(1)}, s32[1,128]{1,0:T(1,128)S(1)}, u32[]{:S(2)}, u32[]{:S(2)}) collective-permute-start(s32[1,128]{1,0:T(1,128)S(1)} %get-tuple-element.12), channel_id=1, source_target_pairs={{0,48},{16,0},{32,16},{48,32},{64,112},{80,64},{96,80},{112,96},{1... | collective-permute-start | bytes 1544 | tf_op jit(solution)/shard_map/ppermute | solution.py:244
  14.2 0.5 %collective-permute-start.1 = (s32[1,128]{1,0:T(1,128)S(1)}, s32[1,128]{1,0:T(1,128)S(1)}, u32[]{:S(2)}, u32[]{:S(2)}) collective-permute-start(s32[1,128]{1,0:T(1,128)S(1)} %get-tuple-element.12), channel_id=1, source_target_pairs={{0,32},{16,48},{32,0},{48,16},{64,96},{80,112},{96,64},{112,80},{1... | collective-permute-start | bytes 1544 | tf_op jit(solution)/shard_map/ppermute | solution.py:244
  14.7 0.6 %collective-permute-start = (s32[1,128]{1,0:T(1,128)S(1)}, s32[1,128]{1,0:T(1,128)S(1)}, u32[]{:S(2)}, u32[]{:S(2)}) collective-permute-start(s32[1,128]{1,0:T(1,128)S(1)} %get-tuple-element.12), channel_id=1, source_target_pairs={{0,16},{16,32},{32,48},{48,0},{64,80},{80,96},{96,112},{112,64},{1... | collective-permute-start | bytes 1544 | tf_op jit(solution)/shard_map/ppermute | solution.py:244
  15.3 0.0 collective-permute-done.2
  15.3 2.9 %collective-permute-done.1 = s32[1,128]{1,0:T(1,128)S(1)} collective-permute-done((s32[1,128]{1,0:T(1,128)S(1)}, s32[1,128]{1,0:T(1,128)S(1)}, u32[]{:S(2)}, u32[]{:S(2)}) %collective-permute-start.1) | collective-permute-done | bytes 544 | tf_op jit(solution)/shard_map/ppermute | solution.py:244
  18.2 0.4 collective-permute-done
  18.6 2.8 %collective-permute-start.5 = (s32[4,128]{1,0:T(4,128)S(1)}, s32[4,128]{1,0:T(4,128)S(1)}, u32[]{:S(2)}, u32[]{:S(2)}) collective-permute-start(s32[4,128]{1,0:T(4,128)S(1)} %pad_add_fusion.refs_0_), channel_id=1, source_target_pairs={{0,192},{16,208},{32,224},{48,240},{64,0},{80,16},{96,32},{112,48}... | collective-permute-start | bytes 6152 | tf_op jit(solution)/shard_map/ppermute | solution.py:246
  21.4 0.3 collective-permute-start.4
  21.8 0.7 %collective-permute-start.3 = (s32[4,128]{1,0:T(4,128)S(1)}, s32[4,128]{1,0:T(4,128)S(1)}, u32[]{:S(2)}, u32[]{:S(2)}) collective-permute-start(s32[4,128]{1,0:T(4,128)S(1)} %pad_add_fusion.refs_0_), channel_id=1, source_target_pairs={{0,64},{16,80},{32,96},{48,112},{64,128},{80,144},{96,160},{112,17... | collective-permute-start | bytes 6152 | tf_op jit(solution)/shard_map/ppermute | solution.py:246
  22.5 0.0 collective-permute-done.5.refs_3_
  22.5 2.9 %collective-permute-done.4.refs_2_ = s32[4,128]{1,0:T(4,128)S(1)} collective-permute-done((s32[4,128]{1,0:T(4,128)S(1)}, s32[4,128]{1,0:T(4,128)S(1)}, u32[]{:S(2)}, u32[]{:S(2)}) %collective-permute-start.4) | collective-permute-done | bytes 2080 | tf_op jit(solution)/shard_map/ppermute | solution.py:246
  25.4 0.1 collective-permute-done.3.refs_1_
  25.4 0.0 all-to-all-done.refs_4_
  25.4 1.7 %pick.1 = bf16[16,120,128]{2,1,0:T(8,128)(2,1)} custom-call(s32[4,128]{1,0:T(4,128)S(1)} %pad_add_fusion.refs_0_, s32[4,128]{1,0:T(4,128)S(1)} %collective-permute-done.3.refs_1_, s32[4,128]{1,0:T(4,128)S(1)} %collective-permute-done.4.refs_2_, s32[4,128]{1,0:T(4,128)S(1)} %collective-permute-done.5.refs_3_, bf16[16,80,128]{2,1,0:T(8,128)(2,1)S(1)} %all-to-all-done.refs_4_), custom_call_target="tpu_custom_call" | custom-call | tf_op jit(solution)/shard_map/pick/pallas_call | solution.py:265
  27.1 6.1 %all-to-all-start.1 = ((bf16[16,120,128]{2,1,0:T(8,128)(2,1)}), bf16[16,120,128]{2,1,0:T(8,128)(2,1)S(1)}, u32[]{:S(2)}, u32[]{:S(2)}) async-start(bf16[16,120,128]{2,1,0:T(8,128)(2,1)} %pick.1), calls=%async_computation.1 | async-start | bytes 983040 | tf_op jit(solution)/shard_map/all_to_all | solution.py:274
  33.2 4.1 %bands.1 = (bf16[3,1536,512]{2,1,0:T(8,128)(2,1)}, f32[12,3,2,128]{3,2,1,0:T(2,128)S(1)}, bf16[256,512]{1,0:T(8,128)(2,1)S(1)}) custom-call(bf16[12,3,2,400]{3,2,1,0:T(2,128)(2,1)} %bitcast.2), custom_call_target="tpu_custom_call" | custom-call | tf_op jit(solution)/shard_map/bands/pallas_call | solution.py:248
  37.4 5.9 %all-to-all-done.1.refs_1_ = bf16[16,120,128]{2,1,0:T(8,128)(2,1)S(1)} async-done(((bf16[16,120,128]{2,1,0:T(8,128)(2,1)}), bf16[16,120,128]{2,1,0:T(8,128)(2,1)S(1)}, u32[]{:S(2)}, u32[]{:S(2)}) %all-to-all-start.1) | async-done | bytes 491552 | tf_op jit(solution)/shard_map/all_to_all | solution.py:274
  43.3 5.9 %correlate.1 = f32[2,768]{1,0:T(2,128)} custom-call(s32[2,128]{1,0:T(2,128)S(1)} %get-tuple-element.11.refs_0_, bf16[16,120,128]{2,1,0:T(8,128)(2,1)S(1)} %all-to-all-done.1.refs_1_, bf16[3,1536,512]{2,1,0:T(8,128)(2,1)} %get-tuple-element.14.refs_2_, f32[12,3,2,128]{3,2,1,0:T(2,128)S(1)} %get-tuple-element.15.refs_3_, ...), custom_call_target="tpu_custom_call" | custom-call | tf_op jit(solution)/shard_map/correlate/pallas_call | solution.py:275
  (1 shorter events, 0.0 us)
Async XLA Ops:
  1.7 23.7 %all-to-all-start = ((bf16[16,80,128]{2,1,0:T(8,128)(2,1)}), bf16[16,80,128]{2,1,0:T(8,128)(2,1)S(1)}, u32[]{:S(2)}, u32[]{:S(2)}) async-start(bf16[16,80,128]{2,1,0:T(8,128)(2,1)} %get-tuple-element.13), calls=%async_computation | async-start | bytes 655360 | tf_op jit(solution)/shard_map/all_to_all | solution.py:247
  11.7 3.6 %collective-permute-start.2 = (s32[1,128]{1,0:T(1,128)S(1)}, s32[1,128]{1,0:T(1,128)S(1)}, u32[]{:S(2)}, u32[]{:S(2)}) collective-permute-start(s32[1,128]{1,0:T(1,128)S(1)} %get-tuple-element.12), channel_id=1, source_target_pairs={{0,48},{16,0},{32,16},{48,32},{64,112},{80,64},{96,80},{112,96},{1... | collective-permute-start | bytes 1544 | tf_op jit(solution)/shard_map/ppermute | solution.py:244
  14.2 4.1 %collective-permute-start.1 = (s32[1,128]{1,0:T(1,128)S(1)}, s32[1,128]{1,0:T(1,128)S(1)}, u32[]{:S(2)}, u32[]{:S(2)}) collective-permute-start(s32[1,128]{1,0:T(1,128)S(1)} %get-tuple-element.12), channel_id=1, source_target_pairs={{0,32},{16,48},{32,0},{48,16},{64,96},{80,112},{96,64},{112,80},{1... | collective-permute-start | bytes 1544 | tf_op jit(solution)/shard_map/ppermute | solution.py:244
  14.7 3.9 %collective-permute-start = (s32[1,128]{1,0:T(1,128)S(1)}, s32[1,128]{1,0:T(1,128)S(1)}, u32[]{:S(2)}, u32[]{:S(2)}) collective-permute-start(s32[1,128]{1,0:T(1,128)S(1)} %get-tuple-element.12), channel_id=1, source_target_pairs={{0,16},{16,32},{32,48},{48,0},{64,80},{80,96},{96,112},{112,64},{1... | collective-permute-start | bytes 1544 | tf_op jit(solution)/shard_map/ppermute | solution.py:244
  18.6 3.9 %collective-permute-start.5 = (s32[4,128]{1,0:T(4,128)S(1)}, s32[4,128]{1,0:T(4,128)S(1)}, u32[]{:S(2)}, u32[]{:S(2)}) collective-permute-start(s32[4,128]{1,0:T(4,128)S(1)} %pad_add_fusion.refs_0_), channel_id=1, source_target_pairs={{0,192},{16,208},{32,224},{48,240},{64,0},{80,16},{96,32},{112,48}... | collective-permute-start | bytes 6152 | tf_op jit(solution)/shard_map/ppermute | solution.py:246
  21.4 3.9 %collective-permute-start.4 = (s32[4,128]{1,0:T(4,128)S(1)}, s32[4,128]{1,0:T(4,128)S(1)}, u32[]{:S(2)}, u32[]{:S(2)}) collective-permute-start(s32[4,128]{1,0:T(4,128)S(1)} %pad_add_fusion.refs_0_), channel_id=1, source_target_pairs={{0,128},{16,144},{32,160},{48,176},{64,192},{80,208},{96,224},{112... | collective-permute-start | bytes 6152 | tf_op jit(solution)/shard_map/ppermute | solution.py:246
  21.8 3.6 %collective-permute-start.3 = (s32[4,128]{1,0:T(4,128)S(1)}, s32[4,128]{1,0:T(4,128)S(1)}, u32[]{:S(2)}, u32[]{:S(2)}) collective-permute-start(s32[4,128]{1,0:T(4,128)S(1)} %pad_add_fusion.refs_0_), channel_id=1, source_target_pairs={{0,64},{16,80},{32,96},{48,112},{64,128},{80,144},{96,160},{112,17... | collective-permute-start | bytes 6152 | tf_op jit(solution)/shard_map/ppermute | solution.py:246
  27.1 16.1 %all-to-all-start.1 = ((bf16[16,120,128]{2,1,0:T(8,128)(2,1)}), bf16[16,120,128]{2,1,0:T(8,128)(2,1)S(1)}, u32[]{:S(2)}, u32[]{:S(2)}) async-start(bf16[16,120,128]{2,1,0:T(8,128)(2,1)} %pick.1), calls=%async_computation.1 | async-start | bytes 983040 | tf_op jit(solution)/shard_map/all_to_all | solution.py:274

commit v4 on v3

--- a/solution.py
+++ b/solution.py
@@ -14,7 +14,9 @@
 TILES = 12
 ROWS = 40
 CAP = 3
-HALF = 64
+PITCH = 48
+STEP = 32
+PHASES = LANES // STEP
 DEPTH = 512
 BLOCKS = WIN // LANES
 SIDE = 4
@@ -58,9 +60,8 @@
         slot_ref[1, e] = shift_ref[e // list_size, e % list_size]
 
 
-def build_bands(templates_ref, band_out, scale_ref, ones_ref, scratch, band_ref, sem):
+def build_bands(shift_ref, templates_ref, band_ref, scale_ref, ones_ref, scratch):
     scratch[...] = jnp.zeros_like(scratch)
-
     list_size = templates_ref.shape[0]
     owned = templates_ref.shape[2]
 
@@ -72,13 +73,11 @@
             scale = lax.rsqrt(energy / TLEN + EPS) / TLEN
             scale_ref[k, c] = jnp.broadcast_to(scale, (owned, LANES))
             for t in range(owned):
-                rows = jnp.broadcast_to(scratch[t : t + 1, :], (HALF, DEPTH))
+                moved = pltpu.roll(scratch[...], shift_ref[t, k] % STEP, 1)
+                rows = jnp.broadcast_to(moved[t : t + 1, :], (STEP, DEPTH))
                 band = pltpu.roll(rows, 0, 1, stride=1, stride_axis=0)
-                place = pl.multiple_of((t * list_size + k) * HALF, HALF)
-                band_ref[c, pl.ds(place, HALF), :] = band.astype(jnp.bfloat16)
-                pltpu.make_async_copy(
-                    band_ref.at[c, pl.ds(place, HALF)], band_out.at[c, pl.ds(place, HALF)], sem
-                ).start()
+                place = pl.multiple_of((t * list_size + k) * STEP, STEP)
+                band_ref[c, pl.ds(place, STEP), :] = band.astype(jnp.bfloat16)
         return carry
 
     lax.fori_loop(0, list_size, step, 0)
@@ -89,7 +88,6 @@
         block = jnp.where(kind, 1.0, 0.0).astype(jnp.bfloat16)
         ones_ref[0:LANES, n * LANES : (n + 1) * LANES] = block
         ones_ref[LANES : 2 * LANES, n * LANES : (n + 1) * LANES] = block
-    pltpu.make_async_copy(band_ref, band_out, sem).wait()
 
 
 def pick(*refs):
@@ -112,24 +110,9 @@
 
 
 def correlate(
-    entries, slot_ref, data_ref, band_in, scale_ref, ones_ref, out_ref,
-    wide, shifted, squares, sums, band_ref, sems,
+    entries, slot_ref, data_ref, band_ref, scale_ref, ones_ref, out_ref,
+    wide, turned, versions, squares, sums,
 ):
-    quads = entries // 4
-    loads = []
-    for quad in range(quads):
-        part = pl.ds(quad * 4 * HALF, 4 * HALF)
-        loads.append(
-            pltpu.make_async_copy(
-                band_in.at[:, part], band_ref.at[:, part], sems.at[quad]
-            )
-        )
-        for c in range(CH):
-            for n in range(1):
-                part = pl.ds(quad * 4 * HALF + n * (4 * HALF // 1), 4 * HALF // 1)
-                pltpu.make_async_copy(
-                    band_in.at[c, part], band_ref.at[c, part], sems.at[quad]
-                ).start()
     groups, rows, _ = data_ref.shape
     list_size = entries // out_ref.shape[0]
     for g in range(groups):
@@ -139,36 +122,44 @@
     lane8 = lax.broadcasted_iota(jnp.int32, (8, LANES), 1)
     for e in range(entries):
         shift = slot_ref[1, e]
-        base = slot_ref[0, e] * ROWS
-        for h in range(2):
-            moved = shift + h * HALF
-            whole = moved // LANES
-            part = moved - whole * LANES
-            back = jnp.where(part == 0, 0, LANES - part)
-            first = pltpu.roll(wide[pl.ds(base + whole, ROWS), :], back, 1)
-            second = pltpu.roll(wide[pl.ds(base + whole + 1, ROWS), :], back, 1)
-            y = jnp.where(lane < LANES - part, first, second)
-            shifted[h, e * ROWS : (e + 1) * ROWS, :] = y
-            if h == 0:
-                sq = y * y
-                high = sq.astype(jnp.bfloat16)
-                squares[e * ROWS : (e + 1) * ROWS, 0:LANES] = high
-                squares[e * ROWS : (e + 1) * ROWS, LANES:] = (
-                    sq - high.astype(jnp.float32)
-                ).astype(jnp.bfloat16)
+        base = pl.multiple_of(slot_ref[0, e] * ROWS, 8)
+        whole = shift // LANES
+        part = shift - whole * LANES
+        back = jnp.where(part == 0, 0, LANES - part)
+        first = pltpu.roll(wide[pl.ds(base + whole, ROWS), :], back, 1)
+        second = pltpu.roll(wide[pl.ds(base + whole + 1, ROWS), :], back, 1)
+        y = jnp.where(lane < LANES - part, first, second)
+        sq = y * y
+        high = sq.astype(jnp.bfloat16)
+        squares[e * ROWS : (e + 1) * ROWS, 0:LANES] = high
+        squares[e * ROWS : (e + 1) * ROWS, LANES:] = (sq - high.astype(jnp.float32)).astype(
+            jnp.bfloat16
+        )
+        record = wide[pl.ds(base, ROWS), :]
+        start = e * PITCH
+        versions[0, start : start + ROWS, :] = record
+        for k in range(1, PHASES):
+            moved = pltpu.roll(record, LANES - k * STEP, 1)
+            turned[k - 1, start : start + ROWS, :] = moved
+            versions[k, start : start + ROWS, :] = jnp.where(
+                lane < LANES - k * STEP, moved, turned[k - 1, start + 1 : start + 1 + ROWS, :]
+            )
     sums[...] = jnp.dot(squares[...], ones_ref[...], preferred_element_type=jnp.float32)
     totals = [jnp.zeros((8, LANES), jnp.float32) for _ in range(out_ref.shape[0])]
-    for quad in range(quads):
-        loads[quad].wait()
+    for batch in range(entries // 8):
         for c in range(CH):
             frames = []
-            for n in range(4):
-                start = (quad * 4 + n) * ROWS + c * TILES
-                for h in range(2):
+            for n in range(8):
+                e = batch * 8 + n
+                coarse = slot_ref[1, e] // STEP
+                for h in range(PHASES):
+                    at = coarse + h
+                    version = at % PHASES
+                    start = e * PITCH + c * TILES + at // PHASES
                     frames.append(
                         jnp.concatenate(
                             [
-                                shifted[h, start + q : start + q + 8, :]
+                                versions[version, pl.ds(start + q, 8), :]
                                 for q in range(DEPTH // LANES)
                             ],
                             axis=1,
@@ -177,20 +168,22 @@
             left = jnp.concatenate(frames, axis=0).astype(jnp.bfloat16)
             product = lax.dot_general(
                 left,
-                band_ref[c, quad * 4 * HALF : (quad + 1) * 4 * HALF, :],
+                band_ref[c, batch * 8 * STEP : (batch + 1) * 8 * STEP, :],
                 (((1,), (1,)), ((), ())),
                 preferred_element_type=jnp.float32,
             )
-            for n in range(4):
-                e = quad * 4 + n
-                column = (n // 2) * LANES
-                low = product[n * 16 : n * 16 + 8, column : column + LANES]
-                high = product[n * 16 + 8 : n * 16 + 16, column : column + LANES]
-                if n % 2 == 0:
-                    high = pltpu.roll(high, HALF, 1)
-                else:
-                    low = pltpu.roll(low, HALF, 1)
-                raw = jnp.where(lane8 < HALF, low, high)
+            for n in range(8):
+                e = batch * 8 + n
+                column = (n // PHASES) * LANES
+                raw = None
+                for h in range(PHASES):
+                    piece = product[
+                        (n * PHASES + h) * 8 : (n * PHASES + h + 1) * 8, column : column + LANES
+                    ]
+                    turn = (h - n) % PHASES * STEP
+                    if turn:
+                        piece = pltpu.roll(piece, turn, 1)
+                    raw = piece if raw is None else jnp.where(lane8 < h * STEP, raw, piece)
                 start = e * ROWS + c * TILES
                 energy = (
                     sums[start : start + 8, 0:LANES]
@@ -217,7 +210,6 @@
     smem = pl.BlockSpec(memory_space=pltpu.SMEM)
     vmem = pl.BlockSpec(memory_space=pltpu.VMEM)
     anywhere = pl.BlockSpec(memory_space=pl.ANY)
-    hbm = pl.BlockSpec(memory_space=pltpu.HBM)
 
     def from_hbm(array):
         return pltpu.with_memory_space_constraint(array, pltpu.HBM)
@@ -248,20 +240,16 @@
     bands, scales, ones = pl.pallas_call(
         build_bands,
         out_shape=(
-            pltpu.HBM((CH, entries * HALF, DEPTH), jnp.bfloat16),
+            jax.ShapeDtypeStruct((CH, entries * STEP, DEPTH), jnp.bfloat16),
             jax.ShapeDtypeStruct((list_size, CH, template_count, LANES), jnp.float32),
             jax.ShapeDtypeStruct((2 * LANES, 4 * LANES), jnp.bfloat16),
         ),
-        in_specs=[vmem],
-        out_specs=(hbm, vmem, vmem),
-        scratch_shapes=[
-            pltpu.VMEM((8, DEPTH), jnp.float32),
-            pltpu.VMEM((CH, entries * HALF, DEPTH), jnp.bfloat16),
-            pltpu.SemaphoreType.DMA,
-        ],
+        in_specs=[smem, vmem],
+        out_specs=(vmem, vmem, vmem),
+        scratch_shapes=[pltpu.VMEM((8, DEPTH), jnp.float32)],
         compiler_params=params(12),
         name="bands",
-    )(from_hbm(jnp.transpose(templates, (1, 2, 0, 3))))
+    )(from_hbm(moveouts), from_hbm(jnp.transpose(templates, (1, 2, 0, 3))))
     picked = pl.pallas_call(
         pick,
         out_shape=jax.ShapeDtypeStruct((groups, CAP * ROWS, LANES), jnp.bfloat16),
@@ -275,19 +263,18 @@
     return pl.pallas_call(
         lambda *refs: correlate(entries, *refs),
         out_shape=jax.ShapeDtypeStruct((template_count, WIN), jnp.float32),
-        in_specs=[smem, vmem, hbm, vmem, vmem],
+        in_specs=[smem, vmem, vmem, vmem, vmem],
         out_specs=vmem,
         scratch_shapes=[
             pltpu.VMEM((groups * CAP * ROWS + 8, LANES), jnp.float32),
-            pltpu.VMEM((2, entries * ROWS, LANES), jnp.float32),
+            pltpu.VMEM((PHASES - 1, entries * PITCH, LANES), jnp.float32),
+            pltpu.VMEM((PHASES, entries * PITCH, LANES), jnp.float32),
             pltpu.VMEM((entries * ROWS, 2 * LANES), jnp.bfloat16),
             pltpu.VMEM((entries * ROWS, 4 * LANES), jnp.float32),
-            pltpu.VMEM((CH, entries * HALF, DEPTH), jnp.bfloat16),
-            pltpu.SemaphoreType.DMA((entries // 4,)),
         ],
-        compiler_params=params(16),
+        compiler_params=params(20),
         name="correlate",
-    )(slots, records, from_hbm(bands), scales, ones)
+    )(slots, records, bands, scales, ones)
 
 
 def solution(mesh):

time: 49.6 us -> 47 us (0.948)
  Pallas kernels: 13.5 us -> 10.6 us
    pallas_call x1, Pallas kernels: 5.95 us -> 3.35 us  [shards(): pl.pallas_call(lambda *refs: correlate(entries, *refs), out_shape=jax.Sha...]
where the time goes in v4:
time: 47 us; the launch traced here: 46.7 us
  starting transfers between devices  23.6 us (50%)
  waiting for transfers between devices  12.5 us (27%)
  Pallas kernels  10.6 us (23%)
    all_to_all x1, starting transfers between devices, shards(): lax.all_to_all(spread, 'tp', split_axis=0, concat_axis=0, tiled=True)  9.99 us
    all_to_all x1, waiting for transfers between devices, shards(): lax.all_to_all(picked, 'st', split_axis=0, concat_axis=0, tiled=True)  6.22 us
    all_to_all x1, starting transfers between devices, shards(): lax.all_to_all(picked, 'st', split_axis=0, concat_axis=0, tiled=True)  6.13 us
    ppermute x3, starting transfers between devices, shards(): lax.ppermute(row, 'st', rotation(d, 0))  3.85 us
    pallas_call x1, Pallas kernels, shards(): pl.pallas_call(build_bands, out_shape=(jax.ShapeDtypeStruct((CH, entries...  3.8 us
    ppermute x3, starting transfers between devices, shards(): lax.ppermute(asked, 'st', rotation(0, d))  3.6 us
    pallas_call x1, Pallas kernels, shards(): pl.pallas_call(lambda *refs: correlate(entries, *refs), out_shape=jax.Sha...  3.35 us
    ppermute x3, waiting for transfers between devices, shards(): lax.ppermute(asked, 'st', rotation(0, d))  3.29 us
  transfers between devices with their start and end apart: 8, of which 5 were waited for; matrix products, arithmetic and copies ran while one was open for 0% of the time, Pallas kernels for 8%

profile of v4, /device:TPU:1, one launch (start us, length us, event | category | flops | bytes accessed | tf_op | source)
XLA Modules:
  0.0 46.7 jit_solution(16745546273358907296)
XLA Ops:
  0.0 1.7 %prepare.1 = (bf16[16,80,128]{2,1,0:T(8,128)(2,1)}, s32[1,128]{1,0:T(1,128)S(1)}, s32[2,128]{1,0:T(2,128)S(1)}) custom-call(s32[2,12]{1,0:T(2,128)} %refs_0_.1, s32[2,12]{1,0:T(2,128)} %shift_ref.1, bf16[3,2,1424]{2,1,0:T(2,128)(2,1)} %bitcast.3), custom_call_target="tpu_custom_call" | custom-call | tf_op jit(solution)/shard_map/prepare/pallas_call | solution.py:220
  1.7 10.0 %all-to-all-start = ((bf16[16,80,128]{2,1,0:T(8,128)(2,1)}), bf16[16,80,128]{2,1,0:T(8,128)(2,1)S(1)}, u32[]{:S(2)}, u32[]{:S(2)}) async-start(bf16[16,80,128]{2,1,0:T(8,128)(2,1)} %get-tuple-element.13), calls=%async_computation | async-start | bytes 655360 | tf_op jit(solution)/shard_map/all_to_all | solution.py:239
  11.7 2.5 %collective-permute-start.2 = (s32[1,128]{1,0:T(1,128)S(1)}, s32[1,128]{1,0:T(1,128)S(1)}, u32[]{:S(2)}, u32[]{:S(2)}) collective-permute-start(s32[1,128]{1,0:T(1,128)S(1)} %get-tuple-element.12), channel_id=1, source_target_pairs={{0,48},{16,0},{32,16},{48,32},{64,112},{80,64},{96,80},{112,96},{1... | collective-permute-start | bytes 1544 | tf_op jit(solution)/shard_map/ppermute | solution.py:236
  14.2 0.5 %collective-permute-start.1 = (s32[1,128]{1,0:T(1,128)S(1)}, s32[1,128]{1,0:T(1,128)S(1)}, u32[]{:S(2)}, u32[]{:S(2)}) collective-permute-start(s32[1,128]{1,0:T(1,128)S(1)} %get-tuple-element.12), channel_id=1, source_target_pairs={{0,32},{16,48},{32,0},{48,16},{64,96},{80,112},{96,64},{112,80},{1... | collective-permute-start | bytes 1544 | tf_op jit(solution)/shard_map/ppermute | solution.py:236
  14.7 0.6 %collective-permute-start = (s32[1,128]{1,0:T(1,128)S(1)}, s32[1,128]{1,0:T(1,128)S(1)}, u32[]{:S(2)}, u32[]{:S(2)}) collective-permute-start(s32[1,128]{1,0:T(1,128)S(1)} %get-tuple-element.12), channel_id=1, source_target_pairs={{0,16},{16,32},{32,48},{48,0},{64,80},{80,96},{96,112},{112,64},{1... | collective-permute-start | bytes 1544 | tf_op jit(solution)/shard_map/ppermute | solution.py:236
  15.3 0.0 collective-permute-done.2
  15.3 2.9 %collective-permute-done.1 = s32[1,128]{1,0:T(1,128)S(1)} collective-permute-done((s32[1,128]{1,0:T(1,128)S(1)}, s32[1,128]{1,0:T(1,128)S(1)}, u32[]{:S(2)}, u32[]{:S(2)}) %collective-permute-start.1) | collective-permute-done | bytes 544 | tf_op jit(solution)/shard_map/ppermute | solution.py:236
  18.2 0.4 collective-permute-done
  18.6 2.8 %collective-permute-start.5 = (s32[4,128]{1,0:T(4,128)S(1)}, s32[4,128]{1,0:T(4,128)S(1)}, u32[]{:S(2)}, u32[]{:S(2)}) collective-permute-start(s32[4,128]{1,0:T(4,128)S(1)} %pad_add_fusion.refs_0_), channel_id=1, source_target_pairs={{0,192},{16,208},{32,224},{48,240},{64,0},{80,16},{96,32},{112,48}... | collective-permute-start | bytes 6152 | tf_op jit(solution)/shard_map/ppermute | solution.py:238
  21.4 0.3 collective-permute-start.4
  21.8 0.7 %collective-permute-start.3 = (s32[4,128]{1,0:T(4,128)S(1)}, s32[4,128]{1,0:T(4,128)S(1)}, u32[]{:S(2)}, u32[]{:S(2)}) collective-permute-start(s32[4,128]{1,0:T(4,128)S(1)} %pad_add_fusion.refs_0_), channel_id=1, source_target_pairs={{0,64},{16,80},{32,96},{48,112},{64,128},{80,144},{96,160},{112,17... | collective-permute-start | bytes 6152 | tf_op jit(solution)/shard_map/ppermute | solution.py:238
  22.5 0.0 collective-permute-done.5.refs_3_
  22.5 2.9 %collective-permute-done.4.refs_2_ = s32[4,128]{1,0:T(4,128)S(1)} collective-permute-done((s32[4,128]{1,0:T(4,128)S(1)}, s32[4,128]{1,0:T(4,128)S(1)}, u32[]{:S(2)}, u32[]{:S(2)}) %collective-permute-start.4) | collective-permute-done | bytes 2080 | tf_op jit(solution)/shard_map/ppermute | solution.py:238
  25.4 0.1 collective-permute-done.3.refs_1_
  25.4 0.0 all-to-all-done.refs_4_
  25.4 1.7 %pick.1 = bf16[16,120,128]{2,1,0:T(8,128)(2,1)} custom-call(s32[4,128]{1,0:T(4,128)S(1)} %pad_add_fusion.refs_0_, s32[4,128]{1,0:T(4,128)S(1)} %collective-permute-done.3.refs_1_, s32[4,128]{1,0:T(4,128)S(1)} %collective-permute-done.4.refs_2_, s32[4,128]{1,0:T(4,128)S(1)} %collective-permute-done.5.refs_3_, bf16[16,80,128]{2,1,0:T(8,128)(2,1)S(1)} %all-to-all-done.refs_4_), custom_call_target="tpu_custom_call" | custom-call | tf_op jit(solution)/shard_map/pick/pallas_call | solution.py:253
  27.1 6.1 %all-to-all-start.1 = ((bf16[16,120,128]{2,1,0:T(8,128)(2,1)}), bf16[16,120,128]{2,1,0:T(8,128)(2,1)S(1)}, u32[]{:S(2)}, u32[]{:S(2)}) async-start(bf16[16,120,128]{2,1,0:T(8,128)(2,1)} %pick.1), calls=%async_computation.1 | async-start | bytes 983040 | tf_op jit(solution)/shard_map/all_to_all | solution.py:262
  33.3 3.8 %bands.1 = (bf16[3,768,512]{2,1,0:T(8,128)(2,1)S(1)}, f32[12,3,2,128]{3,2,1,0:T(2,128)S(1)}, bf16[256,512]{1,0:T(8,128)(2,1)S(1)}) custom-call(s32[2,12]{1,0:T(2,128)} %shift_ref.1, bf16[12,3,2,400]{3,2,1,0:T(2,128)(2,1)} %bitcast.2), custom_call_target="tpu_custom_call" | custom-call | tf_op jit(solution)/shard_map/bands/pallas_call | solution.py:240
  37.1 6.2 %all-to-all-done.1.refs_1_ = bf16[16,120,128]{2,1,0:T(8,128)(2,1)S(1)} async-done(((bf16[16,120,128]{2,1,0:T(8,128)(2,1)}), bf16[16,120,128]{2,1,0:T(8,128)(2,1)S(1)}, u32[]{:S(2)}, u32[]{:S(2)}) %all-to-all-start.1) | async-done | bytes 491552 | tf_op jit(solution)/shard_map/all_to_all | solution.py:262
  43.3 3.4 %correlate.1 = f32[2,768]{1,0:T(2,128)} custom-call(s32[2,128]{1,0:T(2,128)S(1)} %get-tuple-element.11.refs_0_, bf16[16,120,128]{2,1,0:T(8,128)(2,1)S(1)} %all-to-all-done.1.refs_1_, bf16[3,768,512]{2,1,0:T(8,128)(2,1)S(1)} %get-tuple-element.14.refs_2_, f32[12,3,2,128]{3,2,1,0:T(2,128)S(1)} %get-tuple-element.15.refs_3_, ...), custom_call_target="tpu_custom_call" | custom-call | tf_op jit(solution)/shard_map/correlate/pallas_call | solution.py:263
  (1 shorter events, 0.0 us)
Async XLA Ops:
  1.7 23.7 %all-to-all-start = ((bf16[16,80,128]{2,1,0:T(8,128)(2,1)}), bf16[16,80,128]{2,1,0:T(8,128)(2,1)S(1)}, u32[]{:S(2)}, u32[]{:S(2)}) async-start(bf16[16,80,128]{2,1,0:T(8,128)(2,1)} %get-tuple-element.13), calls=%async_computation | async-start | bytes 655360 | tf_op jit(solution)/shard_map/all_to_all | solution.py:239
  11.7 3.6 %collective-permute-start.2 = (s32[1,128]{1,0:T(1,128)S(1)}, s32[1,128]{1,0:T(1,128)S(1)}, u32[]{:S(2)}, u32[]{:S(2)}) collective-permute-start(s32[1,128]{1,0:T(1,128)S(1)} %get-tuple-element.12), channel_id=1, source_target_pairs={{0,48},{16,0},{32,16},{48,32},{64,112},{80,64},{96,80},{112,96},{1... | collective-permute-start | bytes 1544 | tf_op jit(solution)/shard_map/ppermute | solution.py:236
  14.2 4.1 %collective-permute-start.1 = (s32[1,128]{1,0:T(1,128)S(1)}, s32[1,128]{1,0:T(1,128)S(1)}, u32[]{:S(2)}, u32[]{:S(2)}) collective-permute-start(s32[1,128]{1,0:T(1,128)S(1)} %get-tuple-element.12), channel_id=1, source_target_pairs={{0,32},{16,48},{32,0},{48,16},{64,96},{80,112},{96,64},{112,80},{1... | collective-permute-start | bytes 1544 | tf_op jit(solution)/shard_map/ppermute | solution.py:236
  14.7 3.9 %collective-permute-start = (s32[1,128]{1,0:T(1,128)S(1)}, s32[1,128]{1,0:T(1,128)S(1)}, u32[]{:S(2)}, u32[]{:S(2)}) collective-permute-start(s32[1,128]{1,0:T(1,128)S(1)} %get-tuple-element.12), channel_id=1, source_target_pairs={{0,16},{16,32},{32,48},{48,0},{64,80},{80,96},{96,112},{112,64},{1... | collective-permute-start | bytes 1544 | tf_op jit(solution)/shard_map/ppermute | solution.py:236
  18.6 3.9 %collective-permute-start.5 = (s32[4,128]{1,0:T(4,128)S(1)}, s32[4,128]{1,0:T(4,128)S(1)}, u32[]{:S(2)}, u32[]{:S(2)}) collective-permute-start(s32[4,128]{1,0:T(4,128)S(1)} %pad_add_fusion.refs_0_), channel_id=1, source_target_pairs={{0,192},{16,208},{32,224},{48,240},{64,0},{80,16},{96,32},{112,48}... | collective-permute-start | bytes 6152 | tf_op jit(solution)/shard_map/ppermute | solution.py:238
  21.4 3.9 %collective-permute-start.4 = (s32[4,128]{1,0:T(4,128)S(1)}, s32[4,128]{1,0:T(4,128)S(1)}, u32[]{:S(2)}, u32[]{:S(2)}) collective-permute-start(s32[4,128]{1,0:T(4,128)S(1)} %pad_add_fusion.refs_0_), channel_id=1, source_target_pairs={{0,128},{16,144},{32,160},{48,176},{64,192},{80,208},{96,224},{112... | collective-permute-start | bytes 6152 | tf_op jit(solution)/shard_map/ppermute | solution.py:238
  21.8 3.6 %collective-permute-start.3 = (s32[4,128]{1,0:T(4,128)S(1)}, s32[4,128]{1,0:T(4,128)S(1)}, u32[]{:S(2)}, u32[]{:S(2)}) collective-permute-start(s32[4,128]{1,0:T(4,128)S(1)} %pad_add_fusion.refs_0_), channel_id=1, source_target_pairs={{0,64},{16,80},{32,96},{48,112},{64,128},{80,144},{96,160},{112,17... | collective-permute-start | bytes 6152 | tf_op jit(solution)/shard_map/ppermute | solution.py:238
  27.1 16.2 %all-to-all-start.1 = ((bf16[16,120,128]{2,1,0:T(8,128)(2,1)}), bf16[16,120,128]{2,1,0:T(8,128)(2,1)S(1)}, u32[]{:S(2)}, u32[]{:S(2)}) async-start(bf16[16,120,128]{2,1,0:T(8,128)(2,1)} %pick.1), calls=%async_computation.1 | async-start | bytes 983040 | tf_op jit(solution)/shard_map/all_to_all | solution.py:262

commit v5 on v4

--- a/solution.py
+++ b/solution.py
@@ -113,40 +113,44 @@
     entries, slot_ref, data_ref, band_ref, scale_ref, ones_ref, out_ref,
     wide, turned, versions, squares, sums,
 ):
-    groups, rows, _ = data_ref.shape
     list_size = entries // out_ref.shape[0]
-    for g in range(groups):
-        wide[g * rows : (g + 1) * rows, :] = data_ref[g].astype(jnp.float32)
-    wide[groups * rows :, :] = jnp.zeros((wide.shape[0] - groups * rows, LANES), jnp.float32)
     lane = lax.broadcasted_iota(jnp.int32, (ROWS, LANES), 1)
     lane8 = lax.broadcasted_iota(jnp.int32, (8, LANES), 1)
-    for e in range(entries):
-        shift = slot_ref[1, e]
-        base = pl.multiple_of(slot_ref[0, e] * ROWS, 8)
-        whole = shift // LANES
-        part = shift - whole * LANES
-        back = jnp.where(part == 0, 0, LANES - part)
-        first = pltpu.roll(wide[pl.ds(base + whole, ROWS), :], back, 1)
-        second = pltpu.roll(wide[pl.ds(base + whole + 1, ROWS), :], back, 1)
-        y = jnp.where(lane < LANES - part, first, second)
-        sq = y * y
-        high = sq.astype(jnp.bfloat16)
-        squares[e * ROWS : (e + 1) * ROWS, 0:LANES] = high
-        squares[e * ROWS : (e + 1) * ROWS, LANES:] = (sq - high.astype(jnp.float32)).astype(
-            jnp.bfloat16
-        )
-        record = wide[pl.ds(base, ROWS), :]
-        start = e * PITCH
-        versions[0, start : start + ROWS, :] = record
-        for k in range(1, PHASES):
-            moved = pltpu.roll(record, LANES - k * STEP, 1)
-            turned[k - 1, start : start + ROWS, :] = moved
-            versions[k, start : start + ROWS, :] = jnp.where(
-                lane < LANES - k * STEP, moved, turned[k - 1, start + 1 : start + 1 + ROWS, :]
-            )
-    sums[...] = jnp.dot(squares[...], ones_ref[...], preferred_element_type=jnp.float32)
     totals = [jnp.zeros((8, LANES), jnp.float32) for _ in range(out_ref.shape[0])]
     for batch in range(entries // 8):
+        for e in range(batch * 8, batch * 8 + 8):
+            shift = slot_ref[1, e]
+            slot = slot_ref[0, e]
+            group = slot // CAP
+            row = pl.multiple_of((slot - group * CAP) * ROWS, 8)
+            record = data_ref[group, pl.ds(row, ROWS), :].astype(jnp.float32)
+            base = e * PITCH
+            wide[base : base + ROWS, :] = record
+            wide[base + ROWS : base + PITCH, :] = jnp.zeros((PITCH - ROWS, LANES), jnp.float32)
+            whole = shift // LANES
+            part = shift - whole * LANES
+            back = jnp.where(part == 0, 0, LANES - part)
+            first = pltpu.roll(wide[pl.ds(base + whole, ROWS), :], back, 1)
+            second = pltpu.roll(wide[pl.ds(base + whole + 1, ROWS), :], back, 1)
+            y = jnp.where(lane < LANES - part, first, second)
+            sq = y * y
+            high = sq.astype(jnp.bfloat16)
+            squares[e * ROWS : (e + 1) * ROWS, 0:LANES] = high
+            squares[e * ROWS : (e + 1) * ROWS, LANES:] = (sq - high.astype(jnp.float32)).astype(
+                jnp.bfloat16
+            )
+            start = e * PITCH
+            versions[0, start : start + ROWS, :] = record
+            for k in range(1, PHASES):
+                moved = pltpu.roll(record, LANES - k * STEP, 1)
+                turned[k - 1, start : start + ROWS, :] = moved
+                versions[k, start : start + ROWS, :] = jnp.where(
+                    lane < LANES - k * STEP, moved, turned[k - 1, start + 1 : start + 1 + ROWS, :]
+                )
+        part = slice(batch * 8 * ROWS, (batch + 1) * 8 * ROWS)
+        sums[part, :] = jnp.dot(
+            squares[part, :], ones_ref[...], preferred_element_type=jnp.float32
+        )
         for c in range(CH):
             frames = []
             for n in range(8):
@@ -266,7 +270,7 @@
         in_specs=[smem, vmem, vmem, vmem, vmem],
         out_specs=vmem,
         scratch_shapes=[
-            pltpu.VMEM((groups * CAP * ROWS + 8, LANES), jnp.float32),
+            pltpu.VMEM((entries * PITCH, LANES), jnp.float32),
             pltpu.VMEM((PHASES - 1, entries * PITCH, LANES), jnp.float32),
             pltpu.VMEM((PHASES, entries * PITCH, LANES), jnp.float32),
             pltpu.VMEM((entries * ROWS, 2 * LANES), jnp.bfloat16),

time: 47 us -> 46.8 us (level)
  no operation moved by 1% of the time
where the time goes in v5:
time: 46.8 us; the launch traced here: 46.5 us
  starting transfers between devices  23.6 us (50%)
  waiting for transfers between devices  12.5 us (27%)
  Pallas kernels  10.4 us (22%)
    all_to_all x1, starting transfers between devices, shards(): lax.all_to_all(spread, 'tp', split_axis=0, concat_axis=0, tiled=True)  9.99 us
    all_to_all x1, waiting for transfers between devices, shards(): lax.all_to_all(picked, 'st', split_axis=0, concat_axis=0, tiled=True)  6.22 us
    all_to_all x1, starting transfers between devices, shards(): lax.all_to_all(picked, 'st', split_axis=0, concat_axis=0, tiled=True)  6.13 us
    ppermute x3, starting transfers between devices, shards(): lax.ppermute(row, 'st', rotation(d, 0))  3.85 us
    pallas_call x1, Pallas kernels, shards(): pl.pallas_call(build_bands, out_shape=(jax.ShapeDtypeStruct((CH, entries...  3.8 us
    ppermute x3, starting transfers between devices, shards(): lax.ppermute(asked, 'st', rotation(0, d))  3.6 us
    ppermute x3, waiting for transfers between devices, shards(): lax.ppermute(asked, 'st', rotation(0, d))  3.29 us
    pallas_call x1, Pallas kernels, shards(): pl.pallas_call(lambda *refs: correlate(entries, *refs), out_shape=jax.Sha...  3.18 us
  transfers between devices with their start and end apart: 8, of which 5 were waited for; matrix products, arithmetic and copies ran while one was open for 0% of the time, Pallas kernels for 8%

profile of v5, /device:TPU:1, one launch (start us, length us, event | category | flops | bytes accessed | tf_op | source)
XLA Modules:
  0.0 46.5 jit_solution(3328958000179794198)
XLA Ops:
  0.0 1.7 %prepare.1 = (bf16[16,80,128]{2,1,0:T(8,128)(2,1)}, s32[1,128]{1,0:T(1,128)S(1)}, s32[2,128]{1,0:T(2,128)S(1)}) custom-call(s32[2,12]{1,0:T(2,128)} %refs_0_.1, s32[2,12]{1,0:T(2,128)} %shift_ref.1, bf16[3,2,1424]{2,1,0:T(2,128)(2,1)} %bitcast.3), custom_call_target="tpu_custom_call" | custom-call | tf_op jit(solution)/shard_map/prepare/pallas_call | solution.py:224
  1.7 10.0 %all-to-all-start = ((bf16[16,80,128]{2,1,0:T(8,128)(2,1)}), bf16[16,80,128]{2,1,0:T(8,128)(2,1)S(1)}, u32[]{:S(2)}, u32[]{:S(2)}) async-start(bf16[16,80,128]{2,1,0:T(8,128)(2,1)} %get-tuple-element.13), calls=%async_computation | async-start | bytes 655360 | tf_op jit(solution)/shard_map/all_to_all | solution.py:243
  11.7 2.5 %collective-permute-start.2 = (s32[1,128]{1,0:T(1,128)S(1)}, s32[1,128]{1,0:T(1,128)S(1)}, u32[]{:S(2)}, u32[]{:S(2)}) collective-permute-start(s32[1,128]{1,0:T(1,128)S(1)} %get-tuple-element.12), channel_id=1, source_target_pairs={{0,48},{16,0},{32,16},{48,32},{64,112},{80,64},{96,80},{112,96},{1... | collective-permute-start | bytes 1544 | tf_op jit(solution)/shard_map/ppermute | solution.py:240
  14.2 0.5 %collective-permute-start.1 = (s32[1,128]{1,0:T(1,128)S(1)}, s32[1,128]{1,0:T(1,128)S(1)}, u32[]{:S(2)}, u32[]{:S(2)}) collective-permute-start(s32[1,128]{1,0:T(1,128)S(1)} %get-tuple-element.12), channel_id=1, source_target_pairs={{0,32},{16,48},{32,0},{48,16},{64,96},{80,112},{96,64},{112,80},{1... | collective-permute-start | bytes 1544 | tf_op jit(solution)/shard_map/ppermute | solution.py:240
  14.7 0.6 %collective-permute-start = (s32[1,128]{1,0:T(1,128)S(1)}, s32[1,128]{1,0:T(1,128)S(1)}, u32[]{:S(2)}, u32[]{:S(2)}) collective-permute-start(s32[1,128]{1,0:T(1,128)S(1)} %get-tuple-element.12), channel_id=1, source_target_pairs={{0,16},{16,32},{32,48},{48,0},{64,80},{80,96},{96,112},{112,64},{1... | collective-permute-start | bytes 1544 | tf_op jit(solution)/shard_map/ppermute | solution.py:240
  15.3 0.0 collective-permute-done.2
  15.3 2.9 %collective-permute-done.1 = s32[1,128]{1,0:T(1,128)S(1)} collective-permute-done((s32[1,128]{1,0:T(1,128)S(1)}, s32[1,128]{1,0:T(1,128)S(1)}, u32[]{:S(2)}, u32[]{:S(2)}) %collective-permute-start.1) | collective-permute-done | bytes 544 | tf_op jit(solution)/shard_map/ppermute | solution.py:240
  18.2 0.4 collective-permute-done
  18.6 2.8 %collective-permute-start.5 = (s32[4,128]{1,0:T(4,128)S(1)}, s32[4,128]{1,0:T(4,128)S(1)}, u32[]{:S(2)}, u32[]{:S(2)}) collective-permute-start(s32[4,128]{1,0:T(4,128)S(1)} %pad_add_fusion.refs_0_), channel_id=1, source_target_pairs={{0,192},{16,208},{32,224},{48,240},{64,0},{80,16},{96,32},{112,48}... | collective-permute-start | bytes 6152 | tf_op jit(solution)/shard_map/ppermute | solution.py:242
  21.4 0.3 collective-permute-start.4
  21.8 0.7 %collective-permute-start.3 = (s32[4,128]{1,0:T(4,128)S(1)}, s32[4,128]{1,0:T(4,128)S(1)}, u32[]{:S(2)}, u32[]{:S(2)}) collective-permute-start(s32[4,128]{1,0:T(4,128)S(1)} %pad_add_fusion.refs_0_), channel_id=1, source_target_pairs={{0,64},{16,80},{32,96},{48,112},{64,128},{80,144},{96,160},{112,17... | collective-permute-start | bytes 6152 | tf_op jit(solution)/shard_map/ppermute | solution.py:242
  22.5 0.0 collective-permute-done.5.refs_3_
  22.5 2.9 %collective-permute-done.4.refs_2_ = s32[4,128]{1,0:T(4,128)S(1)} collective-permute-done((s32[4,128]{1,0:T(4,128)S(1)}, s32[4,128]{1,0:T(4,128)S(1)}, u32[]{:S(2)}, u32[]{:S(2)}) %collective-permute-start.4) | collective-permute-done | bytes 2080 | tf_op jit(solution)/shard_map/ppermute | solution.py:242
  25.4 0.1 collective-permute-done.3.refs_1_
  25.4 0.0 all-to-all-done.refs_4_
  25.4 1.7 %pick.1 = bf16[16,120,128]{2,1,0:T(8,128)(2,1)} custom-call(s32[4,128]{1,0:T(4,128)S(1)} %pad_add_fusion.refs_0_, s32[4,128]{1,0:T(4,128)S(1)} %collective-permute-done.3.refs_1_, s32[4,128]{1,0:T(4,128)S(1)} %collective-permute-done.4.refs_2_, s32[4,128]{1,0:T(4,128)S(1)} %collective-permute-done.5.refs_3_, bf16[16,80,128]{2,1,0:T(8,128)(2,1)S(1)} %all-to-all-done.refs_4_), custom_call_target="tpu_custom_call" | custom-call | tf_op jit(solution)/shard_map/pick/pallas_call | solution.py:257
  27.1 6.1 %all-to-all-start.1 = ((bf16[16,120,128]{2,1,0:T(8,128)(2,1)}), bf16[16,120,128]{2,1,0:T(8,128)(2,1)S(1)}, u32[]{:S(2)}, u32[]{:S(2)}) async-start(bf16[16,120,128]{2,1,0:T(8,128)(2,1)} %pick.1), calls=%async_computation.1 | async-start | bytes 983040 | tf_op jit(solution)/shard_map/all_to_all | solution.py:266
  33.3 3.8 %bands.1 = (bf16[3,768,512]{2,1,0:T(8,128)(2,1)S(1)}, f32[12,3,2,128]{3,2,1,0:T(2,128)S(1)}, bf16[256,512]{1,0:T(8,128)(2,1)S(1)}) custom-call(s32[2,12]{1,0:T(2,128)} %shift_ref.1, bf16[12,3,2,400]{3,2,1,0:T(2,128)(2,1)} %bitcast.2), custom_call_target="tpu_custom_call" | custom-call | tf_op jit(solution)/shard_map/bands/pallas_call | solution.py:244
  37.1 6.2 %all-to-all-done.1.refs_1_ = bf16[16,120,128]{2,1,0:T(8,128)(2,1)S(1)} async-done(((bf16[16,120,128]{2,1,0:T(8,128)(2,1)}), bf16[16,120,128]{2,1,0:T(8,128)(2,1)S(1)}, u32[]{:S(2)}, u32[]{:S(2)}) %all-to-all-start.1) | async-done | bytes 491552 | tf_op jit(solution)/shard_map/all_to_all | solution.py:266
  43.3 3.2 %correlate.1 = f32[2,768]{1,0:T(2,128)} custom-call(s32[2,128]{1,0:T(2,128)S(1)} %get-tuple-element.11.refs_0_, bf16[16,120,128]{2,1,0:T(8,128)(2,1)S(1)} %all-to-all-done.1.refs_1_, bf16[3,768,512]{2,1,0:T(8,128)(2,1)S(1)} %get-tuple-element.14.refs_2_, f32[12,3,2,128]{3,2,1,0:T(2,128)S(1)} %get-tuple-element.15.refs_3_, ...), custom_call_target="tpu_custom_call" | custom-call | tf_op jit(solution)/shard_map/correlate/pallas_call | solution.py:267
  (1 shorter events, 0.0 us)
Async XLA Ops:
  1.7 23.7 %all-to-all-start = ((bf16[16,80,128]{2,1,0:T(8,128)(2,1)}), bf16[16,80,128]{2,1,0:T(8,128)(2,1)S(1)}, u32[]{:S(2)}, u32[]{:S(2)}) async-start(bf16[16,80,128]{2,1,0:T(8,128)(2,1)} %get-tuple-element.13), calls=%async_computation | async-start | bytes 655360 | tf_op jit(solution)/shard_map/all_to_all | solution.py:243
  11.7 3.6 %collective-permute-start.2 = (s32[1,128]{1,0:T(1,128)S(1)}, s32[1,128]{1,0:T(1,128)S(1)}, u32[]{:S(2)}, u32[]{:S(2)}) collective-permute-start(s32[1,128]{1,0:T(1,128)S(1)} %get-tuple-element.12), channel_id=1, source_target_pairs={{0,48},{16,0},{32,16},{48,32},{64,112},{80,64},{96,80},{112,96},{1... | collective-permute-start | bytes 1544 | tf_op jit(solution)/shard_map/ppermute | solution.py:240
  14.2 4.1 %collective-permute-start.1 = (s32[1,128]{1,0:T(1,128)S(1)}, s32[1,128]{1,0:T(1,128)S(1)}, u32[]{:S(2)}, u32[]{:S(2)}) collective-permute-start(s32[1,128]{1,0:T(1,128)S(1)} %get-tuple-element.12), channel_id=1, source_target_pairs={{0,32},{16,48},{32,0},{48,16},{64,96},{80,112},{96,64},{112,80},{1... | collective-permute-start | bytes 1544 | tf_op jit(solution)/shard_map/ppermute | solution.py:240
  14.7 3.9 %collective-permute-start = (s32[1,128]{1,0:T(1,128)S(1)}, s32[1,128]{1,0:T(1,128)S(1)}, u32[]{:S(2)}, u32[]{:S(2)}) collective-permute-start(s32[1,128]{1,0:T(1,128)S(1)} %get-tuple-element.12), channel_id=1, source_target_pairs={{0,16},{16,32},{32,48},{48,0},{64,80},{80,96},{96,112},{112,64},{1... | collective-permute-start | bytes 1544 | tf_op jit(solution)/shard_map/ppermute | solution.py:240
  18.6 3.9 %collective-permute-start.5 = (s32[4,128]{1,0:T(4,128)S(1)}, s32[4,128]{1,0:T(4,128)S(1)}, u32[]{:S(2)}, u32[]{:S(2)}) collective-permute-start(s32[4,128]{1,0:T(4,128)S(1)} %pad_add_fusion.refs_0_), channel_id=1, source_target_pairs={{0,192},{16,208},{32,224},{48,240},{64,0},{80,16},{96,32},{112,48}... | collective-permute-start | bytes 6152 | tf_op jit(solution)/shard_map/ppermute | solution.py:242
  21.4 3.9 %collective-permute-start.4 = (s32[4,128]{1,0:T(4,128)S(1)}, s32[4,128]{1,0:T(4,128)S(1)}, u32[]{:S(2)}, u32[]{:S(2)}) collective-permute-start(s32[4,128]{1,0:T(4,128)S(1)} %pad_add_fusion.refs_0_), channel_id=1, source_target_pairs={{0,128},{16,144},{32,160},{48,176},{64,192},{80,208},{96,224},{112... | collective-permute-start | bytes 6152 | tf_op jit(solution)/shard_map/ppermute | solution.py:242
  21.8 3.6 %collective-permute-start.3 = (s32[4,128]{1,0:T(4,128)S(1)}, s32[4,128]{1,0:T(4,128)S(1)}, u32[]{:S(2)}, u32[]{:S(2)}) collective-permute-start(s32[4,128]{1,0:T(4,128)S(1)} %pad_add_fusion.refs_0_), channel_id=1, source_target_pairs={{0,64},{16,80},{32,96},{48,112},{64,128},{80,144},{96,160},{112,17... | collective-permute-start | bytes 6152 | tf_op jit(solution)/shard_map/ppermute | solution.py:242
  27.1 16.2 %all-to-all-start.1 = ((bf16[16,120,128]{2,1,0:T(8,128)(2,1)}), bf16[16,120,128]{2,1,0:T(8,128)(2,1)S(1)}, u32[]{:S(2)}, u32[]{:S(2)}) async-start(bf16[16,120,128]{2,1,0:T(8,128)(2,1)} %pick.1), calls=%async_computation.1 | async-start | bytes 983040 | tf_op jit(solution)/shard_map/all_to_all | solution.py:266

commit v6 on v5

--- a/solution.py
+++ b/solution.py
@@ -226,7 +226,7 @@
         out_shape=(
             jax.ShapeDtypeStruct((peers, owned * ROWS, LANES), jnp.bfloat16),
             jax.ShapeDtypeStruct((1, LANES), jnp.int32),
-            jax.ShapeDtypeStruct((2, LANES), jnp.int32),
+            pltpu.SMEM((2, LANES), jnp.int32),
         ),
         in_specs=[smem, smem, vmem],
         out_specs=(vmem, smem, smem),

time: 46.8 us -> 46.4 us (level)
  Pallas kernels: 10.4 us -> 9.93 us
where the time goes in v6:
time: 46.4 us; the launch traced here: 46 us
  starting transfers between devices  23.6 us (51%)
  waiting for transfers between devices  12.5 us (27%)
  Pallas kernels  9.93 us (21%)
    all_to_all x1, starting transfers between devices, shards(): lax.all_to_all(spread, 'tp', split_axis=0, concat_axis=0, tiled=True)  9.99 us
    all_to_all x1, waiting for transfers between devices, shards(): lax.all_to_all(picked, 'st', split_axis=0, concat_axis=0, tiled=True)  6.22 us
    all_to_all x1, starting transfers between devices, shards(): lax.all_to_all(picked, 'st', split_axis=0, concat_axis=0, tiled=True)  6.13 us
    ppermute x3, starting transfers between devices, shards(): lax.ppermute(row, 'st', rotation(d, 0))  3.85 us
    pallas_call x1, Pallas kernels, shards(): pl.pallas_call(build_bands, out_shape=(jax.ShapeDtypeStruct((CH, entries...  3.8 us
    ppermute x3, starting transfers between devices, shards(): lax.ppermute(asked, 'st', rotation(0, d))  3.6 us
    ppermute x3, waiting for transfers between devices, shards(): lax.ppermute(asked, 'st', rotation(0, d))  3.29 us
    ppermute x3, waiting for transfers between devices, shards(): lax.ppermute(row, 'st', rotation(d, 0))  2.95 us
  transfers between devices with their start and end apart: 8, of which 5 were waited for; matrix products, arithmetic and copies ran while one was open for 0% of the time, Pallas kernels for 8%

profile of v6, /device:TPU:1, one launch (start us, length us, event | category | flops | bytes accessed | tf_op | source)
XLA Modules:
  0.0 46.0 jit_solution(2844585248055200107)
XLA Ops:
  0.0 1.7 %prepare.1 = (bf16[16,80,128]{2,1,0:T(8,128)(2,1)}, s32[1,128]{1,0:T(1,128)S(1)}, s32[2,128]{1,0:T(2,128)S(4)}) custom-call(s32[2,12]{1,0:T(2,128)} %refs_0_.1, s32[2,12]{1,0:T(2,128)} %shift_ref.1, bf16[3,2,1424]{2,1,0:T(2,128)(2,1)} %bitcast.3), custom_call_target="tpu_custom_call" | custom-call | tf_op jit(solution)/shard_map/prepare/pallas_call | solution.py:224
  1.7 10.0 %all-to-all-start = ((bf16[16,80,128]{2,1,0:T(8,128)(2,1)}), bf16[16,80,128]{2,1,0:T(8,128)(2,1)S(1)}, u32[]{:S(2)}, u32[]{:S(2)}) async-start(bf16[16,80,128]{2,1,0:T(8,128)(2,1)} %get-tuple-element.13), calls=%async_computation | async-start | bytes 655360 | tf_op jit(solution)/shard_map/all_to_all | solution.py:243
  11.7 2.5 %collective-permute-start.2 = (s32[1,128]{1,0:T(1,128)S(1)}, s32[1,128]{1,0:T(1,128)S(1)}, u32[]{:S(2)}, u32[]{:S(2)}) collective-permute-start(s32[1,128]{1,0:T(1,128)S(1)} %get-tuple-element.12), channel_id=1, source_target_pairs={{0,48},{16,0},{32,16},{48,32},{64,112},{80,64},{96,80},{112,96},{1... | collective-permute-start | bytes 1544 | tf_op jit(solution)/shard_map/ppermute | solution.py:240
  14.2 0.5 %collective-permute-start.1 = (s32[1,128]{1,0:T(1,128)S(1)}, s32[1,128]{1,0:T(1,128)S(1)}, u32[]{:S(2)}, u32[]{:S(2)}) collective-permute-start(s32[1,128]{1,0:T(1,128)S(1)} %get-tuple-element.12), channel_id=1, source_target_pairs={{0,32},{16,48},{32,0},{48,16},{64,96},{80,112},{96,64},{112,80},{1... | collective-permute-start | bytes 1544 | tf_op jit(solution)/shard_map/ppermute | solution.py:240
  14.7 0.6 %collective-permute-start = (s32[1,128]{1,0:T(1,128)S(1)}, s32[1,128]{1,0:T(1,128)S(1)}, u32[]{:S(2)}, u32[]{:S(2)}) collective-permute-start(s32[1,128]{1,0:T(1,128)S(1)} %get-tuple-element.12), channel_id=1, source_target_pairs={{0,16},{16,32},{32,48},{48,0},{64,80},{80,96},{96,112},{112,64},{1... | collective-permute-start | bytes 1544 | tf_op jit(solution)/shard_map/ppermute | solution.py:240
  15.3 0.0 collective-permute-done.2
  15.3 2.9 %collective-permute-done.1 = s32[1,128]{1,0:T(1,128)S(1)} collective-permute-done((s32[1,128]{1,0:T(1,128)S(1)}, s32[1,128]{1,0:T(1,128)S(1)}, u32[]{:S(2)}, u32[]{:S(2)}) %collective-permute-start.1) | collective-permute-done | bytes 544 | tf_op jit(solution)/shard_map/ppermute | solution.py:240
  18.3 0.4 collective-permute-done
  18.6 2.8 %collective-permute-start.5 = (s32[4,128]{1,0:T(4,128)S(1)}, s32[4,128]{1,0:T(4,128)S(1)}, u32[]{:S(2)}, u32[]{:S(2)}) collective-permute-start(s32[4,128]{1,0:T(4,128)S(1)} %pad_add_fusion.refs_0_), channel_id=1, source_target_pairs={{0,192},{16,208},{32,224},{48,240},{64,0},{80,16},{96,32},{112,48}... | collective-permute-start | bytes 6152 | tf_op jit(solution)/shard_map/ppermute | solution.py:242
  21.4 0.3 collective-permute-start.4
  21.8 0.7 %collective-permute-start.3 = (s32[4,128]{1,0:T(4,128)S(1)}, s32[4,128]{1,0:T(4,128)S(1)}, u32[]{:S(2)}, u32[]{:S(2)}) collective-permute-start(s32[4,128]{1,0:T(4,128)S(1)} %pad_add_fusion.refs_0_), channel_id=1, source_target_pairs={{0,64},{16,80},{32,96},{48,112},{64,128},{80,144},{96,160},{112,17... | collective-permute-start | bytes 6152 | tf_op jit(solution)/shard_map/ppermute | solution.py:242
  22.5 0.0 collective-permute-done.5.refs_3_
  22.5 2.9 %collective-permute-done.4.refs_2_ = s32[4,128]{1,0:T(4,128)S(1)} collective-permute-done((s32[4,128]{1,0:T(4,128)S(1)}, s32[4,128]{1,0:T(4,128)S(1)}, u32[]{:S(2)}, u32[]{:S(2)}) %collective-permute-start.4) | collective-permute-done | bytes 2080 | tf_op jit(solution)/shard_map/ppermute | solution.py:242
  25.4 0.1 collective-permute-done.3.refs_1_
  25.4 0.0 all-to-all-done.refs_4_
  25.4 1.7 %pick.1 = bf16[16,120,128]{2,1,0:T(8,128)(2,1)} custom-call(s32[4,128]{1,0:T(4,128)S(1)} %pad_add_fusion.refs_0_, s32[4,128]{1,0:T(4,128)S(1)} %collective-permute-done.3.refs_1_, s32[4,128]{1,0:T(4,128)S(1)} %collective-permute-done.4.refs_2_, s32[4,128]{1,0:T(4,128)S(1)} %collective-permute-done.5.refs_3_, bf16[16,80,128]{2,1,0:T(8,128)(2,1)S(1)} %all-to-all-done.refs_4_), custom_call_target="tpu_custom_call" | custom-call | tf_op jit(solution)/shard_map/pick/pallas_call | solution.py:257
  27.1 6.1 %all-to-all-start.1 = ((bf16[16,120,128]{2,1,0:T(8,128)(2,1)}), bf16[16,120,128]{2,1,0:T(8,128)(2,1)S(1)}, u32[]{:S(2)}, u32[]{:S(2)}) async-start(bf16[16,120,128]{2,1,0:T(8,128)(2,1)} %pick.1), calls=%async_computation.1 | async-start | bytes 983040 | tf_op jit(solution)/shard_map/all_to_all | solution.py:266
  33.3 3.8 %bands.1 = (bf16[3,768,512]{2,1,0:T(8,128)(2,1)S(1)}, f32[12,3,2,128]{3,2,1,0:T(2,128)S(1)}, bf16[256,512]{1,0:T(8,128)(2,1)S(1)}) custom-call(s32[2,12]{1,0:T(2,128)} %shift_ref.1, bf16[12,3,2,400]{3,2,1,0:T(2,128)(2,1)} %bitcast.2), custom_call_target="tpu_custom_call" | custom-call | tf_op jit(solution)/shard_map/bands/pallas_call | solution.py:244
  37.1 6.2 %all-to-all-done.1.refs_1_ = bf16[16,120,128]{2,1,0:T(8,128)(2,1)S(1)} async-done(((bf16[16,120,128]{2,1,0:T(8,128)(2,1)}), bf16[16,120,128]{2,1,0:T(8,128)(2,1)S(1)}, u32[]{:S(2)}, u32[]{:S(2)}) %all-to-all-start.1) | async-done | bytes 491552 | tf_op jit(solution)/shard_map/all_to_all | solution.py:266
  43.3 2.7 %correlate.1 = f32[2,768]{1,0:T(2,128)} custom-call(s32[2,128]{1,0:T(2,128)S(4)} %get-tuple-element.11.refs_0_, bf16[16,120,128]{2,1,0:T(8,128)(2,1)S(1)} %all-to-all-done.1.refs_1_, bf16[3,768,512]{2,1,0:T(8,128)(2,1)S(1)} %get-tuple-element.14.refs_2_, f32[12,3,2,128]{3,2,1,0:T(2,128)S(1)} %get-tuple-element.15.refs_3_, ...), custom_call_target="tpu_custom_call" | custom-call | tf_op jit(solution)/shard_map/correlate/pallas_call | solution.py:267
  (1 shorter events, 0.0 us)
Async XLA Ops:
  1.7 23.7 %all-to-all-start = ((bf16[16,80,128]{2,1,0:T(8,128)(2,1)}), bf16[16,80,128]{2,1,0:T(8,128)(2,1)S(1)}, u32[]{:S(2)}, u32[]{:S(2)}) async-start(bf16[16,80,128]{2,1,0:T(8,128)(2,1)} %get-tuple-element.13), calls=%async_computation | async-start | bytes 655360 | tf_op jit(solution)/shard_map/all_to_all | solution.py:243
  11.7 3.6 %collective-permute-start.2 = (s32[1,128]{1,0:T(1,128)S(1)}, s32[1,128]{1,0:T(1,128)S(1)}, u32[]{:S(2)}, u32[]{:S(2)}) collective-permute-start(s32[1,128]{1,0:T(1,128)S(1)} %get-tuple-element.12), channel_id=1, source_target_pairs={{0,48},{16,0},{32,16},{48,32},{64,112},{80,64},{96,80},{112,96},{1... | collective-permute-start | bytes 1544 | tf_op jit(solution)/shard_map/ppermute | solution.py:240
  14.2 4.1 %collective-permute-start.1 = (s32[1,128]{1,0:T(1,128)S(1)}, s32[1,128]{1,0:T(1,128)S(1)}, u32[]{:S(2)}, u32[]{:S(2)}) collective-permute-start(s32[1,128]{1,0:T(1,128)S(1)} %get-tuple-element.12), channel_id=1, source_target_pairs={{0,32},{16,48},{32,0},{48,16},{64,96},{80,112},{96,64},{112,80},{1... | collective-permute-start | bytes 1544 | tf_op jit(solution)/shard_map/ppermute | solution.py:240
  14.7 3.9 %collective-permute-start = (s32[1,128]{1,0:T(1,128)S(1)}, s32[1,128]{1,0:T(1,128)S(1)}, u32[]{:S(2)}, u32[]{:S(2)}) collective-permute-start(s32[1,128]{1,0:T(1,128)S(1)} %get-tuple-element.12), channel_id=1, source_target_pairs={{0,16},{16,32},{32,48},{48,0},{64,80},{80,96},{96,112},{112,64},{1... | collective-permute-start | bytes 1544 | tf_op jit(solution)/shard_map/ppermute | solution.py:240
  18.6 3.9 %collective-permute-start.5 = (s32[4,128]{1,0:T(4,128)S(1)}, s32[4,128]{1,0:T(4,128)S(1)}, u32[]{:S(2)}, u32[]{:S(2)}) collective-permute-start(s32[4,128]{1,0:T(4,128)S(1)} %pad_add_fusion.refs_0_), channel_id=1, source_target_pairs={{0,192},{16,208},{32,224},{48,240},{64,0},{80,16},{96,32},{112,48}... | collective-permute-start | bytes 6152 | tf_op jit(solution)/shard_map/ppermute | solution.py:242
  21.4 3.9 %collective-permute-start.4 = (s32[4,128]{1,0:T(4,128)S(1)}, s32[4,128]{1,0:T(4,128)S(1)}, u32[]{:S(2)}, u32[]{:S(2)}) collective-permute-start(s32[4,128]{1,0:T(4,128)S(1)} %pad_add_fusion.refs_0_), channel_id=1, source_target_pairs={{0,128},{16,144},{32,160},{48,176},{64,192},{80,208},{96,224},{112... | collective-permute-start | bytes 6152 | tf_op jit(solution)/shard_map/ppermute | solution.py:242
  21.8 3.6 %collective-permute-start.3 = (s32[4,128]{1,0:T(4,128)S(1)}, s32[4,128]{1,0:T(4,128)S(1)}, u32[]{:S(2)}, u32[]{:S(2)}) collective-permute-start(s32[4,128]{1,0:T(4,128)S(1)} %pad_add_fusion.refs_0_), channel_id=1, source_target_pairs={{0,64},{16,80},{32,96},{48,112},{64,128},{80,144},{96,160},{112,17... | collective-permute-start | bytes 6152 | tf_op jit(solution)/shard_map/ppermute | solution.py:242
  27.1 16.2 %all-to-all-start.1 = ((bf16[16,120,128]{2,1,0:T(8,128)(2,1)}), bf16[16,120,128]{2,1,0:T(8,128)(2,1)S(1)}, u32[]{:S(2)}, u32[]{:S(2)}) async-start(bf16[16,120,128]{2,1,0:T(8,128)(2,1)} %pick.1), calls=%async_computation.1 | async-start | bytes 983040 | tf_op jit(solution)/shard_map/all_to_all | solution.py:266

commit v7 on v6

--- a/solution.py
+++ b/solution.py
@@ -90,22 +90,19 @@
         ones_ref[LANES : 2 * LANES, n * LANES : (n + 1) * LANES] = block
 
 
-def pick(*refs):
-    asks, (data_ref, out_ref, sem) = refs[:SIDE], refs[SIDE:]
+def pick(ask_ref, data_ref, out_ref, held, sem):
     me = lax.axis_index("st")
     y, x = me // SIDE, me % SIDE
     for dy in range(SIDE):
         for dx in range(SIDE):
+            n = dy * SIDE + dx
             i = ((y + SIDE - dy) % SIDE) * SIDE + (x + SIDE - dx) % SIDE
             for s in range(CAP):
-                station = asks[dy][dx, me * CAP + s]
+                station = ask_ref[n, me * CAP + s]
                 t = station // 2
-                k = station - t * 2
-                pltpu.make_async_copy(
-                    data_ref.at[t, pl.ds(pl.multiple_of(k * ROWS, 8), ROWS)],
-                    out_ref.at[i, pl.ds(s * ROWS, ROWS)],
-                    sem,
-                ).start()
+                row = pl.multiple_of((station - t * 2) * ROWS, 8)
+                held[n, s * ROWS : (s + 1) * ROWS, :] = data_ref[t, pl.ds(row, ROWS), :]
+            pltpu.make_async_copy(held.at[n], out_ref.at[i], sem).start()
     pltpu.make_async_copy(out_ref, out_ref, sem).wait()
 
 
@@ -257,12 +254,15 @@
     picked = pl.pallas_call(
         pick,
         out_shape=jax.ShapeDtypeStruct((groups, CAP * ROWS, LANES), jnp.bfloat16),
-        in_specs=[smem] * SIDE + [anywhere],
+        in_specs=[smem, vmem],
         out_specs=anywhere,
-        scratch_shapes=[pltpu.SemaphoreType.DMA],
+        scratch_shapes=[
+            pltpu.VMEM((groups, CAP * ROWS, LANES), jnp.bfloat16),
+            pltpu.SemaphoreType.DMA,
+        ],
         compiler_params=params(2),
         name="pick",
-    )(*asks, group_rows)
+    )(jnp.concatenate(asks, axis=0), group_rows)
     records = lax.all_to_all(picked, "st", split_axis=0, concat_axis=0, tiled=True)
     return pl.pallas_call(
         lambda *refs: correlate(entries, *refs),

time: 46.4 us -> 46.3 us (level)
  no operation moved by 1% of the time
where the time goes in v7:
time: 46.3 us; the launch traced here: 46 us
  starting transfers between devices  23.5 us (51%)
  waiting for transfers between devices  12.4 us (27%)
  Pallas kernels  9.92 us (21%)
    all_to_all x1, starting transfers between devices, shards(): lax.all_to_all(spread, 'tp', split_axis=0, concat_axis=0, tiled=True)  9.99 us
    all_to_all x1, waiting for transfers between devices, shards(): lax.all_to_all(picked, 'st', split_axis=0, concat_axis=0, tiled=True)  6.18 us
    all_to_all x1, starting transfers between devices, shards(): lax.all_to_all(picked, 'st', split_axis=0, concat_axis=0, tiled=True)  6.08 us
    ppermute x3, starting transfers between devices, shards(): lax.ppermute(row, 'st', rotation(d, 0))  3.85 us
    pallas_call x1, Pallas kernels, shards(): pl.pallas_call(build_bands, out_shape=(jax.ShapeDtypeStruct((CH, entries...  3.8 us
    ppermute x3, starting transfers between devices, shards(): lax.ppermute(asked, 'st', rotation(0, d))  3.6 us
    ppermute x3, waiting for transfers between devices, shards(): lax.ppermute(asked, 'st', rotation(0, d))  3.29 us
    ppermute x3, waiting for transfers between devices, shards(): lax.ppermute(row, 'st', rotation(d, 0))  2.95 us
  transfers between devices with their start and end apart: 8, of which 5 were waited for; matrix products, arithmetic and copies ran while one was open for 0% of the time, Pallas kernels for 8%

profile of v7, /device:TPU:1, one launch (start us, length us, event | category | flops | bytes accessed | tf_op | source)
XLA Modules:
  0.0 46.0 jit_solution(17415678694209426794)
XLA Ops:
  0.0 1.7 %prepare.1 = (bf16[16,80,128]{2,1,0:T(8,128)(2,1)}, s32[1,128]{1,0:T(1,128)S(1)}, s32[2,128]{1,0:T(2,128)S(4)}) custom-call(s32[2,12]{1,0:T(2,128)} %refs_0_.1, s32[2,12]{1,0:T(2,128)} %shift_ref.1, bf16[3,2,1424]{2,1,0:T(2,128)(2,1)} %bitcast.3), custom_call_target="tpu_custom_call" | custom-call | tf_op jit(solution)/shard_map/prepare/pallas_call | solution.py:221
  1.7 10.0 %all-to-all-start = ((bf16[16,80,128]{2,1,0:T(8,128)(2,1)}), bf16[16,80,128]{2,1,0:T(8,128)(2,1)S(1)}, u32[]{:S(2)}, u32[]{:S(2)}) async-start(bf16[16,80,128]{2,1,0:T(8,128)(2,1)} %get-tuple-element.13), calls=%async_computation | async-start | bytes 655360 | tf_op jit(solution)/shard_map/all_to_all | solution.py:240
  11.7 2.5 %collective-permute-start.2 = (s32[1,128]{1,0:T(1,128)S(1)}, s32[1,128]{1,0:T(1,128)S(1)}, u32[]{:S(2)}, u32[]{:S(2)}) collective-permute-start(s32[1,128]{1,0:T(1,128)S(1)} %get-tuple-element.12), channel_id=1, source_target_pairs={{0,48},{16,0},{32,16},{48,32},{64,112},{80,64},{96,80},{112,96},{1... | collective-permute-start | bytes 1544 | tf_op jit(solution)/shard_map/ppermute | solution.py:237
  14.2 0.5 %collective-permute-start.1 = (s32[1,128]{1,0:T(1,128)S(1)}, s32[1,128]{1,0:T(1,128)S(1)}, u32[]{:S(2)}, u32[]{:S(2)}) collective-permute-start(s32[1,128]{1,0:T(1,128)S(1)} %get-tuple-element.12), channel_id=1, source_target_pairs={{0,32},{16,48},{32,0},{48,16},{64,96},{80,112},{96,64},{112,80},{1... | collective-permute-start | bytes 1544 | tf_op jit(solution)/shard_map/ppermute | solution.py:237
  14.7 0.6 %collective-permute-start = (s32[1,128]{1,0:T(1,128)S(1)}, s32[1,128]{1,0:T(1,128)S(1)}, u32[]{:S(2)}, u32[]{:S(2)}) collective-permute-start(s32[1,128]{1,0:T(1,128)S(1)} %get-tuple-element.12), channel_id=1, source_target_pairs={{0,16},{16,32},{32,48},{48,0},{64,80},{80,96},{96,112},{112,64},{1... | collective-permute-start | bytes 1544 | tf_op jit(solution)/shard_map/ppermute | solution.py:237
  15.3 0.0 collective-permute-done.2
  15.3 2.9 %collective-permute-done.1 = s32[1,128]{1,0:T(1,128)S(1)} collective-permute-done((s32[1,128]{1,0:T(1,128)S(1)}, s32[1,128]{1,0:T(1,128)S(1)}, u32[]{:S(2)}, u32[]{:S(2)}) %collective-permute-start.1) | collective-permute-done | bytes 544 | tf_op jit(solution)/shard_map/ppermute | solution.py:237
  18.3 0.4 collective-permute-done
  18.6 2.8 %collective-permute-start.5 = (s32[4,128]{1,0:T(4,128)S(1)}, s32[4,128]{1,0:T(4,128)S(1)}, u32[]{:S(2)}, u32[]{:S(2)}) collective-permute-start(s32[4,128]{1,0:T(4,128)S(1)} %pad_add_fusion), channel_id=1, source_target_pairs={{0,192},{16,208},{32,224},{48,240},{64,0},{80,16},{96,32},{112,48}... | collective-permute-start | bytes 6152 | tf_op jit(solution)/shard_map/ppermute | solution.py:239
  21.4 0.3 collective-permute-start.4
  21.8 0.7 %collective-permute-start.3 = (s32[4,128]{1,0:T(4,128)S(1)}, s32[4,128]{1,0:T(4,128)S(1)}, u32[]{:S(2)}, u32[]{:S(2)}) collective-permute-start(s32[4,128]{1,0:T(4,128)S(1)} %pad_add_fusion), channel_id=1, source_target_pairs={{0,64},{16,80},{32,96},{48,112},{64,128},{80,144},{96,160},{112,17... | collective-permute-start | bytes 6152 | tf_op jit(solution)/shard_map/ppermute | solution.py:239
  22.5 0.0 collective-permute-done.5
  22.5 2.9 %collective-permute-done.4 = s32[4,128]{1,0:T(4,128)S(1)} collective-permute-done((s32[4,128]{1,0:T(4,128)S(1)}, s32[4,128]{1,0:T(4,128)S(1)}, u32[]{:S(2)}, u32[]{:S(2)}) %collective-permute-start.4) | collective-permute-done | bytes 2080 | tf_op jit(solution)/shard_map/ppermute | solution.py:239
  25.4 0.1 collective-permute-done.3
  25.5 0.0 all-to-all-done.data_ref
  25.5 1.7 %pick.1 = bf16[16,120,128]{2,1,0:T(8,128)(2,1)} custom-call(s32[16,128]{1,0:T(8,128)S(1)} %concatenate.8.ask_ref, bf16[16,80,128]{2,1,0:T(8,128)(2,1)S(1)} %all-to-all-done.data_ref), custom_call_target="tpu_custom_call" | custom-call | tf_op jit(solution)/shard_map/pick/pallas_call | solution.py:254
  27.2 6.1 %all-to-all-start.1 = ((bf16[16,120,128]{2,1,0:T(8,128)(2,1)}), bf16[16,120,128]{2,1,0:T(8,128)(2,1)S(1)}, u32[]{:S(2)}, u32[]{:S(2)}) async-start(bf16[16,120,128]{2,1,0:T(8,128)(2,1)} %pick.1), calls=%async_computation.1 | async-start | bytes 983040 | tf_op jit(solution)/shard_map/all_to_all | solution.py:266
  33.3 3.8 %bands.1 = (bf16[3,768,512]{2,1,0:T(8,128)(2,1)S(1)}, f32[12,3,2,128]{3,2,1,0:T(2,128)S(1)}, bf16[256,512]{1,0:T(8,128)(2,1)S(1)}) custom-call(s32[2,12]{1,0:T(2,128)} %shift_ref.1, bf16[12,3,2,400]{3,2,1,0:T(2,128)(2,1)} %bitcast.2), custom_call_target="tpu_custom_call" | custom-call | tf_op jit(solution)/shard_map/bands/pallas_call | solution.py:241
  37.1 6.2 %all-to-all-done.1.refs_1_ = bf16[16,120,128]{2,1,0:T(8,128)(2,1)S(1)} async-done(((bf16[16,120,128]{2,1,0:T(8,128)(2,1)}), bf16[16,120,128]{2,1,0:T(8,128)(2,1)S(1)}, u32[]{:S(2)}, u32[]{:S(2)}) %all-to-all-start.1) | async-done | bytes 491552 | tf_op jit(solution)/shard_map/all_to_all | solution.py:266
  43.3 2.7 %correlate.1 = f32[2,768]{1,0:T(2,128)} custom-call(s32[2,128]{1,0:T(2,128)S(4)} %get-tuple-element.11.refs_0_, bf16[16,120,128]{2,1,0:T(8,128)(2,1)S(1)} %all-to-all-done.1.refs_1_, bf16[3,768,512]{2,1,0:T(8,128)(2,1)S(1)} %get-tuple-element.14.refs_2_, f32[12,3,2,128]{3,2,1,0:T(2,128)S(1)} %get-tuple-element.15.refs_3_, ...), custom_call_target="tpu_custom_call" | custom-call | tf_op jit(solution)/shard_map/correlate/pallas_call | solution.py:267
  (2 shorter events, 0.1 us)
Async XLA Ops:
  1.7 23.8 %all-to-all-start = ((bf16[16,80,128]{2,1,0:T(8,128)(2,1)}), bf16[16,80,128]{2,1,0:T(8,128)(2,1)S(1)}, u32[]{:S(2)}, u32[]{:S(2)}) async-start(bf16[16,80,128]{2,1,0:T(8,128)(2,1)} %get-tuple-element.13), calls=%async_computation | async-start | bytes 655360 | tf_op jit(solution)/shard_map/all_to_all | solution.py:240
  11.7 3.6 %collective-permute-start.2 = (s32[1,128]{1,0:T(1,128)S(1)}, s32[1,128]{1,0:T(1,128)S(1)}, u32[]{:S(2)}, u32[]{:S(2)}) collective-permute-start(s32[1,128]{1,0:T(1,128)S(1)} %get-tuple-element.12), channel_id=1, source_target_pairs={{0,48},{16,0},{32,16},{48,32},{64,112},{80,64},{96,80},{112,96},{1... | collective-permute-start | bytes 1544 | tf_op jit(solution)/shard_map/ppermute | solution.py:237
  14.2 4.1 %collective-permute-start.1 = (s32[1,128]{1,0:T(1,128)S(1)}, s32[1,128]{1,0:T(1,128)S(1)}, u32[]{:S(2)}, u32[]{:S(2)}) collective-permute-start(s32[1,128]{1,0:T(1,128)S(1)} %get-tuple-element.12), channel_id=1, source_target_pairs={{0,32},{16,48},{32,0},{48,16},{64,96},{80,112},{96,64},{112,80},{1... | collective-permute-start | bytes 1544 | tf_op jit(solution)/shard_map/ppermute | solution.py:237
  14.7 3.9 %collective-permute-start = (s32[1,128]{1,0:T(1,128)S(1)}, s32[1,128]{1,0:T(1,128)S(1)}, u32[]{:S(2)}, u32[]{:S(2)}) collective-permute-start(s32[1,128]{1,0:T(1,128)S(1)} %get-tuple-element.12), channel_id=1, source_target_pairs={{0,16},{16,32},{32,48},{48,0},{64,80},{80,96},{96,112},{112,64},{1... | collective-permute-start | bytes 1544 | tf_op jit(solution)/shard_map/ppermute | solution.py:237
  18.6 3.9 %collective-permute-start.5 = (s32[4,128]{1,0:T(4,128)S(1)}, s32[4,128]{1,0:T(4,128)S(1)}, u32[]{:S(2)}, u32[]{:S(2)}) collective-permute-start(s32[4,128]{1,0:T(4,128)S(1)} %pad_add_fusion), channel_id=1, source_target_pairs={{0,192},{16,208},{32,224},{48,240},{64,0},{80,16},{96,32},{112,48}... | collective-permute-start | bytes 6152 | tf_op jit(solution)/shard_map/ppermute | solution.py:239
  21.4 3.9 %collective-permute-start.4 = (s32[4,128]{1,0:T(4,128)S(1)}, s32[4,128]{1,0:T(4,128)S(1)}, u32[]{:S(2)}, u32[]{:S(2)}) collective-permute-start(s32[4,128]{1,0:T(4,128)S(1)} %pad_add_fusion), channel_id=1, source_target_pairs={{0,128},{16,144},{32,160},{48,176},{64,192},{80,208},{96,224},{112... | collective-permute-start | bytes 6152 | tf_op jit(solution)/shard_map/ppermute | solution.py:239
  21.8 3.6 %collective-permute-start.3 = (s32[4,128]{1,0:T(4,128)S(1)}, s32[4,128]{1,0:T(4,128)S(1)}, u32[]{:S(2)}, u32[]{:S(2)}) collective-permute-start(s32[4,128]{1,0:T(4,128)S(1)} %pad_add_fusion), channel_id=1, source_target_pairs={{0,64},{16,80},{32,96},{48,112},{64,128},{80,144},{96,160},{112,17... | collective-permute-start | bytes 6152 | tf_op jit(solution)/shard_map/ppermute | solution.py:239
  27.2 16.1 %all-to-all-start.1 = ((bf16[16,120,128]{2,1,0:T(8,128)(2,1)}), bf16[16,120,128]{2,1,0:T(8,128)(2,1)S(1)}, u32[]{:S(2)}, u32[]{:S(2)}) async-start(bf16[16,120,128]{2,1,0:T(8,128)(2,1)} %pick.1), calls=%async_computation.1 | async-start | bytes 983040 | tf_op jit(solution)/shard_map/all_to_all | solution.py:266

commit v8 on v7

--- a/solution.py
+++ b/solution.py
@@ -22,9 +22,9 @@
 SIDE = 4
 
 
-def rotation(dy, dx):
+def partners(dy, dx):
     return [
-        (y * SIDE + x, (y + dy) % SIDE * SIDE + (x + dx) % SIDE)
+        (y * SIDE + x, (y ^ dy) * SIDE + (x ^ dx))
         for y in range(SIDE)
         for x in range(SIDE)
     ]
@@ -96,7 +96,7 @@
     for dy in range(SIDE):
         for dx in range(SIDE):
             n = dy * SIDE + dx
-            i = ((y + SIDE - dy) % SIDE) * SIDE + (x + SIDE - dx) % SIDE
+            i = (y ^ dy) * SIDE + (x ^ dx)
             for s in range(CAP):
                 station = ask_ref[n, me * CAP + s]
                 t = station // 2
@@ -234,9 +234,9 @@
         compiler_params=params(4),
         name="prepare",
     )(from_hbm(station_list), from_hbm(moveouts), from_hbm(jnp.swapaxes(continuous, 0, 1)))
-    along_x = [asked] + [lax.ppermute(asked, "st", rotation(0, d)) for d in range(1, SIDE)]
+    along_x = [asked] + [lax.ppermute(asked, "st", partners(0, d)) for d in range(1, SIDE)]
     row = jnp.concatenate(along_x, axis=0)
-    asks = [row] + [lax.ppermute(row, "st", rotation(d, 0)) for d in range(1, SIDE)]
+    asks = [row] + [lax.ppermute(row, "st", partners(d, 0)) for d in range(1, SIDE)]
     group_rows = lax.all_to_all(spread, "tp", split_axis=0, concat_axis=0, tiled=True)
     bands, scales, ones = pl.pallas_call(
         build_bands,

time: 46.3 us -> 46.3 us (level)
    ppermute x6, starting transfers between devices: 7.46 us -> 6.75 us  [the longest x3 3.5 us: shards(): lax.ppermute(row, 'st', partners(d, 0))]
where the time goes in v8:
time: 46.3 us; the launch traced here: 45.9 us
  starting transfers between devices  23.2 us (50%)
  waiting for transfers between devices  12.7 us (27%)
  Pallas kernels  9.9 us (21%)
    all_to_all x1, starting transfers between devices, shards(): lax.all_to_all(spread, 'tp', split_axis=0, concat_axis=0, tiled=True)  9.99 us
    all_to_all x1, starting transfers between devices, shards(): lax.all_to_all(picked, 'st', split_axis=0, concat_axis=0, tiled=True)  6.49 us
    all_to_all x1, waiting for transfers between devices, shards(): lax.all_to_all(picked, 'st', split_axis=0, concat_axis=0, tiled=True)  6.16 us
    pallas_call x1, Pallas kernels, shards(): pl.pallas_call(build_bands, out_shape=(jax.ShapeDtypeStruct((CH, entries...  3.8 us
    ppermute x3, starting transfers between devices, shards(): lax.ppermute(row, 'st', partners(d, 0))  3.5 us
    ppermute x3, waiting for transfers between devices, shards(): lax.ppermute(asked, 'st', partners(0, d))  3.29 us
    ppermute x3, waiting for transfers between devices, shards(): lax.ppermute(row, 'st', partners(d, 0))  3.26 us
    ppermute x3, starting transfers between devices, shards(): lax.ppermute(asked, 'st', partners(0, d))  3.25 us
  transfers between devices with their start and end apart: 8, of which 5 were waited for; matrix products, arithmetic and copies ran while one was open for 0% of the time, Pallas kernels for 8%

profile of v8, /device:TPU:1, one launch (start us, length us, event | category | flops | bytes accessed | tf_op | source)
XLA Modules:
  0.0 45.9 jit_solution(879190363009619181)
XLA Ops:
  0.0 1.7 %prepare.1 = (bf16[16,80,128]{2,1,0:T(8,128)(2,1)}, s32[1,128]{1,0:T(1,128)S(1)}, s32[2,128]{1,0:T(2,128)S(4)}) custom-call(s32[2,12]{1,0:T(2,128)} %refs_0_.1, s32[2,12]{1,0:T(2,128)} %shift_ref.1, bf16[3,2,1424]{2,1,0:T(2,128)(2,1)} %bitcast.3), custom_call_target="tpu_custom_call" | custom-call | tf_op jit(solution)/shard_map/prepare/pallas_call | solution.py:221
  1.7 10.0 %all-to-all-start = ((bf16[16,80,128]{2,1,0:T(8,128)(2,1)}), bf16[16,80,128]{2,1,0:T(8,128)(2,1)S(1)}, u32[]{:S(2)}, u32[]{:S(2)}) async-start(bf16[16,80,128]{2,1,0:T(8,128)(2,1)} %get-tuple-element.13), calls=%async_computation | async-start | bytes 655360 | tf_op jit(solution)/shard_map/all_to_all | solution.py:240
  11.7 2.5 %collective-permute-start.2 = (s32[1,128]{1,0:T(1,128)S(1)}, s32[1,128]{1,0:T(1,128)S(1)}, u32[]{:S(2)}, u32[]{:S(2)}) collective-permute-start(s32[1,128]{1,0:T(1,128)S(1)} %get-tuple-element.12), channel_id=1, source_target_pairs={{0,48},{16,32},{32,16},{48,0},{64,112},{80,96},{96,80},{112,64},{1... | collective-permute-start | bytes 1544 | tf_op jit(solution)/shard_map/ppermute | solution.py:237
  14.2 0.5 %collective-permute-start.1 = (s32[1,128]{1,0:T(1,128)S(1)}, s32[1,128]{1,0:T(1,128)S(1)}, u32[]{:S(2)}, u32[]{:S(2)}) collective-permute-start(s32[1,128]{1,0:T(1,128)S(1)} %get-tuple-element.12), channel_id=1, source_target_pairs={{0,32},{16,48},{32,0},{48,16},{64,96},{80,112},{96,64},{112,80},{1... | collective-permute-start | bytes 1544 | tf_op jit(solution)/shard_map/ppermute | solution.py:237
  14.7 0.3 collective-permute-start
  15.0 0.3 collective-permute-done.2
  15.3 2.9 %collective-permute-done.1 = s32[1,128]{1,0:T(1,128)S(1)} collective-permute-done((s32[1,128]{1,0:T(1,128)S(1)}, s32[1,128]{1,0:T(1,128)S(1)}, u32[]{:S(2)}, u32[]{:S(2)}) %collective-permute-start.1) | collective-permute-done | bytes 544 | tf_op jit(solution)/shard_map/ppermute | solution.py:237
  18.3 0.0 collective-permute-done
  18.3 2.8 %collective-permute-start.5 = (s32[4,128]{1,0:T(4,128)S(1)}, s32[4,128]{1,0:T(4,128)S(1)}, u32[]{:S(2)}, u32[]{:S(2)}) collective-permute-start(s32[4,128]{1,0:T(4,128)S(1)} %pad_add_fusion), channel_id=1, source_target_pairs={{0,192},{16,208},{32,224},{48,240},{64,128},{80,144},{96,160},{112... | collective-permute-start | bytes 6152 | tf_op jit(solution)/shard_map/ppermute | solution.py:239
  21.1 0.3 collective-permute-start.4
  21.4 0.3 collective-permute-start.3
  21.8 0.3 collective-permute-done.5
  22.1 3.0 %collective-permute-done.4 = s32[4,128]{1,0:T(4,128)S(1)} collective-permute-done((s32[4,128]{1,0:T(4,128)S(1)}, s32[4,128]{1,0:T(4,128)S(1)}, u32[]{:S(2)}, u32[]{:S(2)}) %collective-permute-start.4) | collective-permute-done | bytes 2080 | tf_op jit(solution)/shard_map/ppermute | solution.py:239
  25.0 0.0 collective-permute-done.3
  25.1 0.0 all-to-all-done.data_ref
  25.1 1.7 %pick.1 = bf16[16,120,128]{2,1,0:T(8,128)(2,1)} custom-call(s32[16,128]{1,0:T(8,128)S(1)} %concatenate.8.ask_ref, bf16[16,80,128]{2,1,0:T(8,128)(2,1)S(1)} %all-to-all-done.data_ref), custom_call_target="tpu_custom_call" | custom-call | tf_op jit(solution)/shard_map/pick/pallas_call | solution.py:254
  26.8 6.5 %all-to-all-start.1 = ((bf16[16,120,128]{2,1,0:T(8,128)(2,1)}), bf16[16,120,128]{2,1,0:T(8,128)(2,1)S(1)}, u32[]{:S(2)}, u32[]{:S(2)}) async-start(bf16[16,120,128]{2,1,0:T(8,128)(2,1)} %pick.1), calls=%async_computation.1 | async-start | bytes 983040 | tf_op jit(solution)/shard_map/all_to_all | solution.py:266
  33.3 3.8 %bands.1 = (bf16[3,768,512]{2,1,0:T(8,128)(2,1)S(1)}, f32[12,3,2,128]{3,2,1,0:T(2,128)S(1)}, bf16[256,512]{1,0:T(8,128)(2,1)S(1)}) custom-call(s32[2,12]{1,0:T(2,128)} %shift_ref.1, bf16[12,3,2,400]{3,2,1,0:T(2,128)(2,1)} %bitcast.2), custom_call_target="tpu_custom_call" | custom-call | tf_op jit(solution)/shard_map/bands/pallas_call | solution.py:241
  37.1 6.2 %all-to-all-done.1.refs_1_ = bf16[16,120,128]{2,1,0:T(8,128)(2,1)S(1)} async-done(((bf16[16,120,128]{2,1,0:T(8,128)(2,1)}), bf16[16,120,128]{2,1,0:T(8,128)(2,1)S(1)}, u32[]{:S(2)}, u32[]{:S(2)}) %all-to-all-start.1) | async-done | bytes 491552 | tf_op jit(solution)/shard_map/all_to_all | solution.py:266
  43.2 2.7 %correlate.1 = f32[2,768]{1,0:T(2,128)} custom-call(s32[2,128]{1,0:T(2,128)S(4)} %get-tuple-element.11.refs_0_, bf16[16,120,128]{2,1,0:T(8,128)(2,1)S(1)} %all-to-all-done.1.refs_1_, bf16[3,768,512]{2,1,0:T(8,128)(2,1)S(1)} %get-tuple-element.14.refs_2_, f32[12,3,2,128]{3,2,1,0:T(2,128)S(1)} %get-tuple-element.15.refs_3_, ...), custom_call_target="tpu_custom_call" | custom-call | tf_op jit(solution)/shard_map/correlate/pallas_call | solution.py:267
  (2 shorter events, 0.1 us)
Async XLA Ops:
  1.7 23.4 %all-to-all-start = ((bf16[16,80,128]{2,1,0:T(8,128)(2,1)}), bf16[16,80,128]{2,1,0:T(8,128)(2,1)S(1)}, u32[]{:S(2)}, u32[]{:S(2)}) async-start(bf16[16,80,128]{2,1,0:T(8,128)(2,1)} %get-tuple-element.13), calls=%async_computation | async-start | bytes 655360 | tf_op jit(solution)/shard_map/all_to_all | solution.py:240
  11.7 3.6 %collective-permute-start.2 = (s32[1,128]{1,0:T(1,128)S(1)}, s32[1,128]{1,0:T(1,128)S(1)}, u32[]{:S(2)}, u32[]{:S(2)}) collective-permute-start(s32[1,128]{1,0:T(1,128)S(1)} %get-tuple-element.12), channel_id=1, source_target_pairs={{0,48},{16,32},{32,16},{48,0},{64,112},{80,96},{96,80},{112,64},{1... | collective-permute-start | bytes 1544 | tf_op jit(solution)/shard_map/ppermute | solution.py:237
  14.2 4.1 %collective-permute-start.1 = (s32[1,128]{1,0:T(1,128)S(1)}, s32[1,128]{1,0:T(1,128)S(1)}, u32[]{:S(2)}, u32[]{:S(2)}) collective-permute-start(s32[1,128]{1,0:T(1,128)S(1)} %get-tuple-element.12), channel_id=1, source_target_pairs={{0,32},{16,48},{32,0},{48,16},{64,96},{80,112},{96,64},{112,80},{1... | collective-permute-start | bytes 1544 | tf_op jit(solution)/shard_map/ppermute | solution.py:237
  14.7 3.5 %collective-permute-start = (s32[1,128]{1,0:T(1,128)S(1)}, s32[1,128]{1,0:T(1,128)S(1)}, u32[]{:S(2)}, u32[]{:S(2)}) collective-permute-start(s32[1,128]{1,0:T(1,128)S(1)} %get-tuple-element.12), channel_id=1, source_target_pairs={{0,16},{16,0},{32,48},{48,32},{64,80},{80,64},{96,112},{112,96},{1... | collective-permute-start | bytes 1544 | tf_op jit(solution)/shard_map/ppermute | solution.py:237
  18.3 3.8 %collective-permute-start.5 = (s32[4,128]{1,0:T(4,128)S(1)}, s32[4,128]{1,0:T(4,128)S(1)}, u32[]{:S(2)}, u32[]{:S(2)}) collective-permute-start(s32[4,128]{1,0:T(4,128)S(1)} %pad_add_fusion), channel_id=1, source_target_pairs={{0,192},{16,208},{32,224},{48,240},{64,128},{80,144},{96,160},{112... | collective-permute-start | bytes 6152 | tf_op jit(solution)/shard_map/ppermute | solution.py:239
  21.1 3.9 %collective-permute-start.4 = (s32[4,128]{1,0:T(4,128)S(1)}, s32[4,128]{1,0:T(4,128)S(1)}, u32[]{:S(2)}, u32[]{:S(2)}) collective-permute-start(s32[4,128]{1,0:T(4,128)S(1)} %pad_add_fusion), channel_id=1, source_target_pairs={{0,128},{16,144},{32,160},{48,176},{64,192},{80,208},{96,224},{112... | collective-permute-start | bytes 6152 | tf_op jit(solution)/shard_map/ppermute | solution.py:239
  21.4 3.6 %collective-permute-start.3 = (s32[4,128]{1,0:T(4,128)S(1)}, s32[4,128]{1,0:T(4,128)S(1)}, u32[]{:S(2)}, u32[]{:S(2)}) collective-permute-start(s32[4,128]{1,0:T(4,128)S(1)} %pad_add_fusion), channel_id=1, source_target_pairs={{0,64},{16,80},{32,96},{48,112},{64,0},{80,16},{96,32},{112,48},{1... | collective-permute-start | bytes 6152 | tf_op jit(solution)/shard_map/ppermute | solution.py:239
  26.8 16.5 %all-to-all-start.1 = ((bf16[16,120,128]{2,1,0:T(8,128)(2,1)}), bf16[16,120,128]{2,1,0:T(8,128)(2,1)S(1)}, u32[]{:S(2)}, u32[]{:S(2)}) async-start(bf16[16,120,128]{2,1,0:T(8,128)(2,1)} %pick.1), calls=%async_computation.1 | async-start | bytes 983040 | tf_op jit(solution)/shard_map/all_to_all | solution.py:266
